TPU v7x, 32 devices: a whole 2x2x4 slice. The times are simulated.
32 devices in a mesh: tm: 8 (over z, y), swath: 4 (over x, core).
Axes of the slice: x: 2, y: 2, z: 4, core: 2. Of those that a mesh axis runs over, the one named last changes fastest.
Arguments:
- design: bfloat16 [8, 2048, 512], P('tm', 'swath'), may hold values from -6 to 6
- process: bfloat16 [8, 512, 512], P('tm', 'swath')
- prior_prec: float32 [8, 512], P('tm', 'swath'), may hold values from 0.05 to 0.5
- routes: int32 [8, 16], P('tm', 'swath'), may hold values from -1 to 7, as said below
- counts: int32 [8, 4], P('tm', 'swath'), may hold values from 1 to 4
Outputs:
- reduced_diag: float32 [8, 512, 512], P('tm', 'swath')
- reduced_coupling: float32 [8, 512, 512], P('tm', 'swath')
Inputs may be any that keep to these rules, and one draw needn't show every extreme that they name: `routes`: each value is the holder's own time block i or i + 1, or -1 only where i + 1 would be 8; of one holder's 4 blocks, exactly 2 name i and the others i + 1 or -1.
All inputs are finite; a program needn't handle non-finite values.
Results may differ from a plain program's by a relative error of at most 0.00073.
Values may be sent and summed in bfloat16 or wider, within the bound.
A program may use at most 64 MiB of HBM per device.

v0:
```python
import jax
import jax.numpy as jnp
from jax import lax
from jax.sharding import PartitionSpec as P

LEVELS = 3


def passed_along(block, axis, distance):
    devices = range(lax.axis_size(axis))
    route = [(i - distance, i) for i in devices if i - distance in devices]
    return lax.ppermute(block, axis, route)


def tri_solve(factor, right):
    return lax.linalg.triangular_solve(factor, right, left_side=True, lower=True)


def inner_rows(left_side, right_side):
    return lax.dot_general(
        left_side,
        right_side,
        (((0,), (0,)), ((), ())),
        precision=lax.Precision.HIGHEST,
        preferred_element_type=jnp.float32,
    )


def compact(scaled, wanted, slot_count):
    sort_key = jnp.where(wanted, 0, 1).astype(jnp.int32)
    picked = jnp.argsort(sort_key, stable=True)[:slot_count]
    kept = jnp.take(sort_key, picked) == 0
    return jnp.where(kept[:, None, None], scaled[picked], 0.0).astype(jnp.bfloat16)


def shards(design, process, prior_prec, routes, counts):
    row_count = process.shape[1]
    order_size = process.shape[2]
    time_count = lax.axis_size("tm")
    my_time = lax.axis_index("tm")
    swath_index = lax.axis_index("swath")
    block_count = routes.shape[1]
    slot_count = block_count // 2
    block_rows = design.shape[1] // block_count
    total_slots = 2 * slot_count * block_rows * lax.axis_size("swath")
    row_start = swath_index * row_count
    raw_rows = design[0].reshape(block_count, block_rows, order_size).astype(jnp.float32)
    mean_sq = jnp.mean(raw_rows * raw_rows, axis=-1, keepdims=True)
    scaled = raw_rows * lax.rsqrt(4.0 * total_slots * (mean_sq + 1e-06))
    live = jnp.arange(block_count) < counts[0, 0]
    target = routes[0]
    own_blocks = compact(scaled, live & (target == my_time), slot_count)
    ahead_blocks = compact(scaled, live & (target == my_time + 1), slot_count)
    incoming, previous = passed_along((ahead_blocks, process), "tm", 1)
    gram_input = jnp.concatenate([own_blocks, incoming], axis=0).reshape(-1, order_size)
    shard_rows = lax.all_gather(gram_input, "swath", axis=0, tiled=True)
    columns = lax.dynamic_slice_in_dim(shard_rows, row_start, row_count, 1)
    gram = lax.dot_general(
        columns, shard_rows, (((0,), (0,)), ((), ())), preferred_element_type=jnp.float32
    )
    unit_rows = jnp.arange(order_size)[None, :] == jnp.arange(row_count)[:, None] + row_start
    diag_rows = previous[0].astype(jnp.float32) + process[0].astype(jnp.float32) + gram
    diag_rows = diag_rows + jnp.where(unit_rows, prior_prec[0][:, None], 0.0)
    coup_rows = -process[0].astype(jnp.float32)
    unit_full = jnp.eye(order_size, dtype=jnp.float32)
    for level in range(LEVELS):
        distance = 2**level
        full_diag, full_coup = (
            lax.all_gather(diag_rows, "swath", axis=0, tiled=True),
            lax.all_gather(coup_rows, "swath", axis=0, tiled=True),
        )
        factor = jnp.linalg.cholesky(full_diag)
        solved = tri_solve(factor, full_coup)
        own_cols = lax.dynamic_slice_in_dim(solved, row_start, row_count, 1)
        eliminated = inner_rows(own_cols, solved)
        left_term = passed_along(eliminated, "tm", distance)
        factor_part = lax.dynamic_slice_in_dim(factor, row_start, row_count, 0)
        solved_part = lax.dynamic_slice_in_dim(solved, row_start, row_count, 0)
        moved = passed_along((factor_part, solved_part), "tm", -distance)
        far_factor, far_solved = (
            lax.all_gather(moved[0], "swath", axis=0, tiled=True),
            lax.all_gather(moved[1], "swath", axis=0, tiled=True),
        )
        has_partner = my_time + distance < time_count
        far_factor = jnp.where(has_partner, far_factor, unit_full)
        cross = tri_solve(far_factor, full_coup.T)
        cross_cols = lax.dynamic_slice_in_dim(cross, row_start, row_count, 1)
        right_term = inner_rows(cross_cols, cross)
        new_coupling = inner_rows(cross_cols, far_solved)
        diag_rows = diag_rows - left_term - jnp.where(has_partner, right_term, 0.0)
        coup_rows = -new_coupling
    return (diag_rows[None], coup_rows[None])


def solution(mesh):
    return jax.shard_map(
        shards,
        mesh=mesh,
        in_specs=(
            P("tm", "swath", None),
            P("tm", "swath", None),
            P("tm", "swath"),
            P("tm", "swath"),
            P("tm", "swath"),
        ),
        out_specs=(P("tm", "swath", None), P("tm", "swath", None)),
        check_vma=False,
    )
```

profile of v0, /device:TPU:0, one launch (start us, length us, event | category | flops | bytes accessed | tf_op | source)
XLA Modules:
  0.0 771.1 jit_solution(9951725097706804160)
XLA Ops:
  32.3 17.8 %all-gather.15.cloned.1.call-done = bf16[2048,512]{1,0:T(8,128)(2,1)} async-done(((bf16[512,512]{1,0:T(8,128)(2,1)}), bf16[2048,512]{1,0:T(8,128)(2,1)}) %all-gather.15.cloned.1.call-update) | async-done | bytes 2097168 | tf_op jit(solution)/shard_map/all_gather | solution.py:56
  54.3 16.1 %all-gather.17.cloned.1.call-done = f32[512,512]{0,1:T(8,128)} async-done(((f32[128,512]{0,1:T(8,128)}), f32[512,512]{0,1:T(8,128)}) %all-gather.17.cloned.1.call-update) | async-done | bytes 1048592 | tf_op jit(solution)/shard_map/all_gather | solution.py:69
  72.3 11.7 %cholesky.374 = f32[128,128]{1,0:T(8,128)S(1)} custom-call(f32[128,128]{1,0:T(8,128)S(1)} %cholesky.586), custom_call_target="Cholesky" | custom-call | tf_op jit(solution)/shard_map/jit(cholesky)/cholesky | solution.py:72
  84.2 9.8 %custom-call.34 = f32[1,128,128]{1,2,0:T(8,128)S(1)} custom-call(f32[1,128,128]{2,1,0:T(8,128)S(1)} %get-tuple-element.152), custom_call_target="InvertDiagBlocksLowerTriangular" | custom-call | tf_op jit(solution)/shard_map/jit(cholesky)/cholesky | solution.py:72
  94.7 11.7 %cholesky.393 = f32[128,128]{1,0:T(8,128)S(1)} custom-call(f32[128,128]{1,0:T(8,128)S(1)} %cholesky.590), custom_call_target="Cholesky" | custom-call | tf_op jit(solution)/shard_map/jit(cholesky)/cholesky | solution.py:72
  106.5 10.2 %custom-call.35 = f32[1,128,128]{1,2,0:T(8,128)S(1)} custom-call(f32[1,128,128]{2,1,0:T(8,128)S(1)} %get-tuple-element.149), custom_call_target="InvertDiagBlocksLowerTriangular" | custom-call | tf_op jit(solution)/shard_map/jit(cholesky)/cholesky | solution.py:72
  117.4 11.7 %cholesky.414 = f32[128,128]{1,0:T(8,128)S(1)} custom-call(f32[128,128]{1,0:T(8,128)S(1)} %cholesky.595), custom_call_target="Cholesky" | custom-call | tf_op jit(solution)/shard_map/jit(cholesky)/cholesky | solution.py:72
  129.1 9.8 %custom-call.36 = f32[1,128,128]{1,2,0:T(8,128)S(1)} custom-call(f32[1,128,128]{2,1,0:T(8,128)S(1)} %get-tuple-element.146), custom_call_target="InvertDiagBlocksLowerTriangular" | custom-call | tf_op jit(solution)/shard_map/jit(cholesky)/cholesky | solution.py:72
  139.6 11.7 %cholesky.431 = f32[128,128]{1,0:T(8,128)S(1)} custom-call(f32[128,128]{1,0:T(8,128)S(1)} %convolution_subtract_fusion.20), custom_call_target="Cholesky" | custom-call | tf_op jit(solution)/shard_map/jit(cholesky)/cholesky | solution.py:72
  164.5 39.9 %custom-call.37 = f32[4,128,128]{1,2,0:T(8,128)} custom-call(f32[4,128,128]{2,1,0:T(8,128)S(1)} %get-tuple-element.47), custom_call_target="InvertDiagBlocksLowerTriangular" | custom-call | tf_op jit(solution)/shard_map/triangular_solve/custom-call.3 | solution.py:16
  243.3 39.3 %custom-call.38 = f32[4,128,128]{1,2,0:T(8,128)S(1)} custom-call(f32[4,128,128]{2,1,0:T(8,128)S(1)} %get-tuple-element.48), custom_call_target="InvertDiagBlocksLowerTriangular" | custom-call | tf_op jit(solution)/shard_map/triangular_solve/custom-call.3 | solution.py:16
  291.7 12.9 %all-gather.21.cloned.1.call-done = f32[512,512]{0,1:T(8,128)} async-done(((f32[128,512]{0,1:T(8,128)}), f32[512,512]{0,1:T(8,128)}) %all-gather.21.cloned.1.call-update) | async-done | bytes 1048592 | tf_op jit(solution)/shard_map/all_gather | solution.py:69
  306.5 11.7 %cholesky.446 = f32[128,128]{1,0:T(8,128)S(1)} custom-call(f32[128,128]{1,0:T(8,128)S(1)} %cholesky.599), custom_call_target="Cholesky" | custom-call | tf_op jit(solution)/shard_map/jit(cholesky)/cholesky | solution.py:72
  318.4 9.8 %custom-call.39 = f32[1,128,128]{1,2,0:T(8,128)S(1)} custom-call(f32[1,128,128]{2,1,0:T(8,128)S(1)} %get-tuple-element.142), custom_call_target="InvertDiagBlocksLowerTriangular" | custom-call | tf_op jit(solution)/shard_map/jit(cholesky)/cholesky | solution.py:72
  328.9 11.7 %cholesky.465 = f32[128,128]{1,0:T(8,128)S(1)} custom-call(f32[128,128]{1,0:T(8,128)S(1)} %cholesky.603), custom_call_target="Cholesky" | custom-call | tf_op jit(solution)/shard_map/jit(cholesky)/cholesky | solution.py:72
  340.6 10.0 %custom-call.40 = f32[1,128,128]{1,2,0:T(8,128)S(1)} custom-call(f32[1,128,128]{2,1,0:T(8,128)S(1)} %get-tuple-element.139), custom_call_target="InvertDiagBlocksLowerTriangular" | custom-call | tf_op jit(solution)/shard_map/jit(cholesky)/cholesky | solution.py:72
  351.3 11.7 %cholesky.486 = f32[128,128]{1,0:T(8,128)S(1)} custom-call(f32[128,128]{1,0:T(8,128)S(1)} %cholesky.608), custom_call_target="Cholesky" | custom-call | tf_op jit(solution)/shard_map/jit(cholesky)/cholesky | solution.py:72
  363.0 9.8 %custom-call.41 = f32[1,128,128]{1,2,0:T(8,128)S(1)} custom-call(f32[1,128,128]{2,1,0:T(8,128)S(1)} %get-tuple-element.136), custom_call_target="InvertDiagBlocksLowerTriangular" | custom-call | tf_op jit(solution)/shard_map/jit(cholesky)/cholesky | solution.py:72
  373.4 11.7 %cholesky.503 = f32[128,128]{1,0:T(8,128)S(1)} custom-call(f32[128,128]{1,0:T(8,128)S(1)} %convolution_subtract_fusion.19), custom_call_target="Cholesky" | custom-call | tf_op jit(solution)/shard_map/jit(cholesky)/cholesky | solution.py:72
  399.2 39.3 %custom-call.42 = f32[4,128,128]{1,2,0:T(8,128)S(1)} custom-call(f32[4,128,128]{2,1,0:T(8,128)S(1)} %get-tuple-element.49), custom_call_target="InvertDiagBlocksLowerTriangular" | custom-call | tf_op jit(solution)/shard_map/triangular_solve/custom-call.3 | solution.py:16
  475.5 39.3 %custom-call.43 = f32[4,128,128]{1,2,0:T(8,128)S(1)} custom-call(f32[4,128,128]{2,1,0:T(8,128)S(1)} %get-tuple-element.50), custom_call_target="InvertDiagBlocksLowerTriangular" | custom-call | tf_op jit(solution)/shard_map/triangular_solve/custom-call.3 | solution.py:16
  525.3 13.0 %all-gather.29.cloned.1.call-done = f32[512,512]{0,1:T(8,128)} async-done(((f32[128,512]{0,1:T(8,128)}), f32[512,512]{0,1:T(8,128)}) %all-gather.29.cloned.1.call-update) | async-done | bytes 1048592 | tf_op jit(solution)/shard_map/all_gather | solution.py:69
  540.2 11.7 %cholesky.518 = f32[128,128]{1,0:T(8,128)S(1)} custom-call(f32[128,128]{1,0:T(8,128)S(1)} %cholesky.612), custom_call_target="Cholesky" | custom-call | tf_op jit(solution)/shard_map/jit(cholesky)/cholesky | solution.py:72
  552.1 9.8 %custom-call.44 = f32[1,128,128]{1,2,0:T(8,128)S(1)} custom-call(f32[1,128,128]{2,1,0:T(8,128)S(1)} %get-tuple-element.132), custom_call_target="InvertDiagBlocksLowerTriangular" | custom-call | tf_op jit(solution)/shard_map/jit(cholesky)/cholesky | solution.py:72
  562.6 11.7 %cholesky.537 = f32[128,128]{1,0:T(8,128)S(1)} custom-call(f32[128,128]{1,0:T(8,128)S(1)} %cholesky.616), custom_call_target="Cholesky" | custom-call | tf_op jit(solution)/shard_map/jit(cholesky)/cholesky | solution.py:72
  574.3 10.0 %custom-call.45 = f32[1,128,128]{1,2,0:T(8,128)S(1)} custom-call(f32[1,128,128]{2,1,0:T(8,128)S(1)} %get-tuple-element.129), custom_call_target="InvertDiagBlocksLowerTriangular" | custom-call | tf_op jit(solution)/shard_map/jit(cholesky)/cholesky | solution.py:72
  585.0 11.7 %cholesky.558 = f32[128,128]{1,0:T(8,128)S(1)} custom-call(f32[128,128]{1,0:T(8,128)S(1)} %cholesky.621), custom_call_target="Cholesky" | custom-call | tf_op jit(solution)/shard_map/jit(cholesky)/cholesky | solution.py:72
  596.8 9.8 %custom-call.46 = f32[1,128,128]{1,2,0:T(8,128)S(1)} custom-call(f32[1,128,128]{2,1,0:T(8,128)S(1)} %get-tuple-element.126), custom_call_target="InvertDiagBlocksLowerTriangular" | custom-call | tf_op jit(solution)/shard_map/jit(cholesky)/cholesky | solution.py:72
  607.2 11.7 %cholesky.575 = f32[128,128]{1,0:T(8,128)S(1)} custom-call(f32[128,128]{1,0:T(8,128)S(1)} %convolution_subtract_fusion.18), custom_call_target="Cholesky" | custom-call | tf_op jit(solution)/shard_map/jit(cholesky)/cholesky | solution.py:72
  633.1 39.3 %custom-call.47 = f32[4,128,128]{1,2,0:T(8,128)S(1)} custom-call(f32[4,128,128]{2,1,0:T(8,128)S(1)} %get-tuple-element.51), custom_call_target="InvertDiagBlocksLowerTriangular" | custom-call | tf_op jit(solution)/shard_map/triangular_solve/custom-call.3 | solution.py:16
  675.7 13.7 %collective-permute-done.9 = f32[128,512]{1,0:T(8,128)S(1)} collective-permute-done((f32[128,512]{1,0:T(8,128)S(1)}, f32[128,512]{1,0:T(8,128)S(1)}, u32[]{:S(2)}, u32[]{:S(2)}) %collective-permute-start.9) | collective-permute-done | bytes 262176 | tf_op jit(solution)/shard_map/ppermute | solution.py:12
  714.8 39.3 %custom-call.48 = f32[4,128,128]{1,2,0:T(8,128)S(1)} custom-call(f32[4,128,128]{2,1,0:T(8,128)S(1)} %get-tuple-element.52), custom_call_target="InvertDiagBlocksLowerTriangular" | custom-call | tf_op jit(solution)/shard_map/triangular_solve/custom-call.3 | solution.py:16
  (340 shorter events, 256.1 us)
Async XLA Ops:
  7.2 43.0 %all-gather.15.cloned.1.call-start = ((), (), s32[]{:S(2)}) async-start(), calls=%async_computation | async-start | bytes 2621440 | tf_op jit(solution)/shard_map/all_gather | solution.py:56
  13.1 12.1 %copy-start.20 = (bf16[1,128,512]{2,1,0:T(8,128)(2,1)S(1)}, bf16[1,128,512]{2,1,0:T(8,128)(2,1)}, u32[]{:S(2)}) copy-start(bf16[1,128,512]{2,1,0:T(8,128)(2,1)} %param.11) | copy-start | bytes 393220
  13.7 36.4 %copy-start.21 = (f32[1,128]{1,0:T(1,128)S(1)}, f32[1,128]{1,0:T(1,128)}, u32[]{:S(2)}) copy-start(f32[1,128]{1,0:T(1,128)} %param.12) | copy-start | bytes 1540
  13.9 10.5 %collective-permute-start.1 = (bf16[2,128,512]{2,1,0:T(8,128)(2,1)S(1)}, bf16[2,128,512]{2,1,0:T(8,128)(2,1)S(1)}, u32[]{:S(2)}, u32[]{:S(2)}) collective-permute-start(bf16[2,128,512]{2,1,0:T(8,128)(2,1)S(1)} %select_convert_fusion), channel_id=1, source_target_pairs={{0,4},{4,8},{8,12},{12,16},{16,20},{20,24},{24,28},{1,5},{5,9},{9,... | collective-permute-start | bytes 786440 | tf_op jit(solution)/shard_map/ppermute | solution.py:12
  25.2 45.2 %all-gather.17.cloned.1.call-start = ((), (), s32[]{:S(2)}) async-start(), calls=%async_computation.1 | async-start | bytes 1310720 | tf_op jit(solution)/shard_map/all_gather | solution.py:69
  25.4 6.9 collective-permute-start
  53.5 153.2 %all-gather.39.cloned.1.call-start = ((), (), s32[]{:S(2)}) async-start(), calls=%async_computation.12 | async-start | bytes 1310720 | tf_op jit(solution)/shard_map/all_gather | solution.py:70
  54.3 179.1 %all-gather.19.cloned.1.call-start = ((), (), s32[]{:S(2)}) async-start(), calls=%async_computation.2 | async-start | bytes 1310720 | tf_op jit(solution)/shard_map/all_gather | solution.py:81
  205.2 13.7 %copy-start.9 = (f32[4,128,128]{1,2,0:T(8,128)S(1)}, f32[4,128,128]{1,2,0:T(8,128)}, u32[]{:S(2)}) copy-start(f32[4,128,128]{1,2,0:T(8,128)} %custom-call.37) | copy-start | bytes 786436
  205.2 10.7 %collective-permute-start.3 = (f32[128,512]{1,0:T(8,128)}, f32[128,512]{1,0:T(8,128)S(1)}, u32[]{:S(2)}, u32[]{:S(2)}) collective-permute-start(f32[128,512]{1,0:T(8,128)} %constant_dynamic-slice_fusion.11), channel_id=1, source_target_pairs={{4,0},{8,4},{12,8},{16,12},{20,16},{24,20},{28,24},{5,1},{9,5},{13... | collective-permute-start | bytes 786440 | tf_op jit(solution)/shard_map/ppermute | solution.py:12
  206.6 11.3 %copy-start.3 = (f32[1,512,512]{1,2,0:T(8,128)S(1)}, f32[1,512,512]{1,2,0:T(8,128)}, u32[]{:S(2)}) copy-start(f32[1,512,512]{1,2,0:T(8,128)} %all-gather.39.cloned.1.call-done) | copy-start | bytes 3145732
  216.6 71.9 %all-gather.23.cloned.1.call-start = ((), (), s32[]{:S(2)}) async-start(), calls=%async_computation.4 | async-start | bytes 1310720 | tf_op jit(solution)/shard_map/all_gather | solution.py:82
  221.4 10.1 %collective-permute-start.4 = (f32[128,512]{1,0:T(8,128)S(1)}, f32[128,512]{1,0:T(8,128)S(1)}, u32[]{:S(2)}, u32[]{:S(2)}) collective-permute-start(f32[128,512]{1,0:T(8,128)S(1)} %constant_dynamic-slice_fusion.10), channel_id=1, source_target_pairs={{4,0},{8,4},{12,8},{16,12},{20,16},{24,20},{28,24},{5,1},{9,5},{13... | collective-permute-start | bytes 786440 | tf_op jit(solution)/shard_map/ppermute | solution.py:12
  224.5 61.4 %collective-permute-start.2 = (f32[128,512]{0,1:T(8,128)S(1)}, f32[128,512]{0,1:T(8,128)S(1)}, u32[]{:S(2)}, u32[]{:S(2)}) collective-permute-start(f32[128,512]{0,1:T(8,128)S(1)} %fusion.93), channel_id=1, source_target_pairs={{0,4},{4,8},{8,12},{12,16},{16,20},{20,24},{24,28},{1,5},{5,9},{9,... | collective-permute-start | bytes 786440 | tf_op jit(solution)/shard_map/ppermute | solution.py:12
  232.2 72.4 %all-gather.21.cloned.1.call-start = ((), (), s32[]{:S(2)}) async-start(), calls=%async_computation.3 | async-start | bytes 1310720 | tf_op jit(solution)/shard_map/all_gather | solution.py:69
  288.4 151.5 %all-gather.25.cloned.1.call-start = ((), (), s32[]{:S(2)}) async-start(), calls=%async_computation.5 | async-start | bytes 1310720 | tf_op jit(solution)/shard_map/all_gather | solution.py:70
  291.2 174.4 %all-gather.27.cloned.1.call-start = ((), (), s32[]{:S(2)}) async-start(), calls=%async_computation.6 | async-start | bytes 1310720 | tf_op jit(solution)/shard_map/all_gather | solution.py:81
  438.6 10.3 %collective-permute-start.6 = (f32[128,512]{1,0:T(8,128)S(1)}, f32[128,512]{1,0:T(8,128)S(1)}, u32[]{:S(2)}, u32[]{:S(2)}) collective-permute-start(f32[128,512]{1,0:T(8,128)S(1)} %constant_dynamic-slice_fusion.9), channel_id=1, source_target_pairs={{8,0},{12,4},{16,8},{20,12},{24,16},{28,20},{9,1},{13,5},{17,9},{2... | collective-permute-start | bytes 786440 | tf_op jit(solution)/shard_map/ppermute | solution.py:12
  439.9 11.6 %copy-start.5 = (f32[512,512]{1,0:T(8,128)S(1)}, f32[512,512]{1,0:T(8,128)}, u32[]{:S(2)}) copy-start(f32[512,512]{1,0:T(8,128)} %all-gather.25.cloned.1.call-done) | copy-start | bytes 3145732
  441.4 10.2 %copy-start.17 = (f32[4,128,128]{1,2,0:T(8,128)S(1)}, f32[4,128,128]{1,2,0:T(8,128)}, u32[]{:S(2)}) copy-start(f32[4,128,128]{1,2,0:T(8,128)} %copy-done.16) | copy-start | bytes 786436
  449.7 72.7 %all-gather.31.cloned.1.call-start = ((), (), s32[]{:S(2)}) async-start(), calls=%async_computation.8 | async-start | bytes 1310720 | tf_op jit(solution)/shard_map/all_gather | solution.py:82
  453.2 9.5 %collective-permute-start.7 = (f32[128,512]{1,0:T(8,128)S(1)}, f32[128,512]{1,0:T(8,128)S(1)}, u32[]{:S(2)}, u32[]{:S(2)}) collective-permute-start(f32[128,512]{1,0:T(8,128)S(1)} %constant_dynamic-slice_fusion.8), channel_id=1, source_target_pairs={{8,0},{12,4},{16,8},{20,12},{24,16},{28,20},{9,1},{13,5},{17,9},{2... | collective-permute-start | bytes 786440 | tf_op jit(solution)/shard_map/ppermute | solution.py:12
  456.3 63.4 %collective-permute-start.5 = (f32[128,512]{0,1:T(8,128)S(1)}, f32[128,512]{0,1:T(8,128)S(1)}, u32[]{:S(2)}, u32[]{:S(2)}) collective-permute-start(f32[128,512]{0,1:T(8,128)S(1)} %fusion.91), channel_id=1, source_target_pairs={{0,8},{4,12},{8,16},{12,20},{16,24},{20,28},{1,9},{5,13},{9,17},{1... | collective-permute-start | bytes 786440 | tf_op jit(solution)/shard_map/ppermute | solution.py:12
  463.4 74.9 %all-gather.29.cloned.1.call-start = ((), (), s32[]{:S(2)}) async-start(), calls=%async_computation.7 | async-start | bytes 1310720 | tf_op jit(solution)/shard_map/all_gather | solution.py:69
  522.2 151.6 %all-gather.33.cloned.1.call-start = ((), (), s32[]{:S(2)}) async-start(), calls=%async_computation.9 | async-start | bytes 1310720 | tf_op jit(solution)/shard_map/all_gather | solution.py:70
  525.0 180.7 %all-gather.35.cloned.1.call-start = ((), (), s32[]{:S(2)}) async-start(), calls=%async_computation.10 | async-start | bytes 1310720 | tf_op jit(solution)/shard_map/all_gather | solution.py:81
  672.5 16.9 %collective-permute-start.9 = (f32[128,512]{1,0:T(8,128)S(1)}, f32[128,512]{1,0:T(8,128)S(1)}, u32[]{:S(2)}, u32[]{:S(2)}) collective-permute-start(f32[128,512]{1,0:T(8,128)S(1)} %constant_dynamic-slice_fusion.7), channel_id=1, source_target_pairs={{16,0},{20,4},{24,8},{28,12},{17,1},{21,5},{25,9},{29,13},{18,2},{... | collective-permute-start | bytes 786440 | tf_op jit(solution)/shard_map/ppermute | solution.py:12
  673.9 18.1 %copy-start.4 = (f32[512,512]{1,0:T(8,128)S(1)}, f32[512,512]{1,0:T(8,128)}, u32[]{:S(2)}) copy-start(f32[512,512]{1,0:T(8,128)} %all-gather.33.cloned.1.call-done) | copy-start | bytes 3145732
  675.3 16.7 %copy-start.19 = (f32[4,128,128]{1,2,0:T(8,128)S(1)}, f32[4,128,128]{1,2,0:T(8,128)}, u32[]{:S(2)}) copy-start(f32[4,128,128]{1,2,0:T(8,128)} %copy-done.18) | copy-start | bytes 786436
  690.1 71.6 %all-gather.37.cloned.1.call-start = ((), (), s32[]{:S(2)}) async-start(), calls=%async_computation.11 | async-start | bytes 1310720 | tf_op jit(solution)/shard_map/all_gather | solution.py:82
  693.6 11.3 %collective-permute-start.10 = (f32[128,512]{1,0:T(8,128)S(1)}, f32[128,512]{1,0:T(8,128)S(1)}, u32[]{:S(2)}, u32[]{:S(2)}) collective-permute-start(f32[128,512]{1,0:T(8,128)S(1)} %constant_dynamic-slice_fusion.6), channel_id=1, source_target_pairs={{16,0},{20,4},{24,8},{28,12},{17,1},{21,5},{25,9},{29,13},{18,2},{... | collective-permute-start | bytes 786440 | tf_op jit(solution)/shard_map/ppermute | solution.py:12
  696.8 62.3 %collective-permute-start.8 = (f32[128,512]{0,1:T(8,128)S(1)}, f32[128,512]{0,1:T(8,128)S(1)}, u32[]{:S(2)}, u32[]{:S(2)}) collective-permute-start(f32[128,512]{0,1:T(8,128)S(1)} %fusion.89), channel_id=1, source_target_pairs={{0,16},{4,20},{8,24},{12,28},{1,17},{5,21},{9,25},{13,29},{2,18},{... | collective-permute-start | bytes 786440 | tf_op jit(solution)/shard_map/ppermute | solution.py:12
  (14 other events, 17.1 us)
Sparse Core Ops, SparseCore 0:
  25.3 24.7 all-gather.14
  53.6 16.8 all-gather.16
  72.6 16.9 all-gather.38
  216.7 16.6 all-gather.18
  234.8 16.7 all-gather.22
  288.5 16.0 all-gather.20
  306.7 16.7 all-gather.24
  449.8 15.7 all-gather.26
  467.2 16.7 all-gather.30
  522.4 15.8 all-gather.28
  540.4 16.7 all-gather.32
  690.2 13.9 all-gather.34
  705.8 16.6 all-gather.36
where the time goes:
time: 783 us; the launch traced here: 771 us
  other arithmetic  488 us (62%)
  waiting for transfers between devices  103 us (13%)
  local copies, waits for them, and re-layouts  62.4 us (8%)
  matrix products  59.8 us (8%)
  starting transfers between devices  33.8 us (4%)
  between operations  23.7 us (3%)
    another operation x19, other arithmetic, tri_solve(): lax.linalg.triangular_solve(factor, right, left_side=True, lower=True)  243 us
    another operation x45, other arithmetic, shards(): factor = jnp.linalg.cholesky(full_diag)  238 us
    another operation x79, local copies, waits for them, and re-layouts, tri_solve(): lax.linalg.triangular_solve(factor, right, left_side=True, lower=True)  48.5 us
    all_gather x3, waiting for transfers between devices, shards(): lax.all_gather(diag_rows, 'swath', axis=0, tiled=True)  42.1 us
    ppermute x11, waiting for transfers between devices, passed_along(): return lax.ppermute(block, axis, route)  40.1 us
    ppermute x11, starting transfers between devices, passed_along(): return lax.ppermute(block, axis, route)  32.3 us
    another operation x42, matrix products, tri_solve(): lax.linalg.triangular_solve(factor, right, left_side=True, lower=True)  30.5 us
    dot_general x9, matrix products, inner_rows(): lax.dot_general(left_side, right_side, (((0,), (0,)), ((), ())), precisio...  20.4 us
  transfers between devices with their start and end apart: 24, of which 14 were waited for; matrix products, arithmetic and copies ran while one was open for 77% of the time, Pallas kernels for 0%

commit v1 on v0

v1 whole, which is shorter than its diff:
```python
import functools

import jax
import jax.numpy as jnp
from jax import lax
from jax.experimental import pallas as pl
from jax.experimental.pallas import tpu as pltpu
from jax.sharding import PartitionSpec as P

LEVELS = 3


def passed_along(block, axis, distance):
    devices = range(lax.axis_size(axis))
    route = [(i - distance, i) for i in devices if i - distance in devices]
    return lax.ppermute(block, axis, route)


def split(x):
    high = x.astype(jnp.bfloat16)
    return high, (x - high.astype(jnp.float32)).astype(jnp.bfloat16)


def dot3(a, b, left):
    (ah, al), (bh, bl) = a, b
    dot = functools.partial(
        lax.dot_general,
        dimension_numbers=(((left,), (0,)), ((), ())),
        preferred_element_type=jnp.float32,
    )
    return dot(ah, bh) + (dot(ah, bl) + dot(al, bh))


def factor_inverse(m):
    n = m.shape[0]
    groups = n // 8
    rows = [m[8 * g : 8 * g + 8, :] for g in range(groups)]
    lane = lax.broadcasted_iota(jnp.int32, (8, n), 1)
    sub = lax.broadcasted_iota(jnp.int32, (8, n), 0)
    for j in range(n):
        g, s = divmod(j, 8)
        row = rows[g][s : s + 1, :]
        r = lax.rsqrt(row[:, j : j + 1])
        pivot_row = jnp.broadcast_to(jnp.where(lane[:1] == j, 1.0, row) * r, (8, n))
        here = lane == j
        for h in range(g, groups):
            if h == g and s == 7:
                continue
            column = rows[h][:, j : j + 1] * r
            new = jnp.where(here, 0.0, rows[h]) - column * pivot_row
            rows[h] = jnp.where(sub > s, new, rows[h]) if h == g else new
        rows[g] = jnp.where(sub == s, pivot_row, rows[g])
    out = jnp.concatenate(rows, axis=0)
    down = lax.broadcasted_iota(jnp.int32, (n, n), 0)
    across = lax.broadcasted_iota(jnp.int32, (n, n), 1)
    return jnp.where(down >= across, out, 0.0)


def level_kernel(index_ref, parts_ref, up_ref, down_ref, work, high, low):
    blocks, _, rows, order = parts_ref.shape
    wide = work.shape[2]
    for i in range(blocks):
        for part in range(3):
            work[i, :, part * order : (part + 1) * order] = parts_ref[i, part]
    for i in range(blocks):
        for k in range(i, blocks):
            here = work[i, :, k * rows : (k + 1) * rows]
            there = work[k, :, i * rows : (i + 1) * rows]
            work[i, :, k * rows : (k + 1) * rows] = 0.5 * (here + there.T)

    def step(j, carry):
        at = pl.ds(pl.multiple_of(j * rows, rows), rows)
        inverse = factor_inverse(work[j, :, at])
        solved = dot3(split(inverse), split(work[j]), 1)
        solved_high, solved_low = split(solved)
        high[at, :] = solved_high
        low[at, :] = solved_low
        for i in range(1, blocks):

            @pl.when(i > j)
            def _():
                cut = slice(i * rows, (i + 1) * rows)
                left = (high[at, cut], low[at, cut])
                work[i] = work[i] - dot3(left, (solved_high, solved_low), 0)

        return carry

    lax.fori_loop(0, blocks, step, 0)
    mine = index_ref[0] * rows
    for out_ref, base in ((up_ref, order), (down_ref, 2 * order)):
        cut = pl.ds(pl.multiple_of(base + mine, rows), rows)
        left = (high[:, cut], low[:, cut])
        for half in range(2):
            right = slice((1 + half) * order, (2 + half) * order)
            out_ref[:, half * order : (half + 1) * order] = dot3(
                left, (high[:, right], low[:, right]), 0
            )


def eliminate(index, parts):
    blocks, _, rows, order = parts.shape
    out = jax.ShapeDtypeStruct((rows, 2 * order), jnp.float32)
    return pl.pallas_call(
        level_kernel,
        out_shape=(out, out),
        in_specs=[
            pl.BlockSpec(memory_space=pltpu.SMEM),
            pl.BlockSpec(memory_space=pltpu.VMEM),
        ],
        out_specs=(pl.BlockSpec(memory_space=pltpu.VMEM),) * 2,
        scratch_shapes=[
            pltpu.VMEM((blocks, rows, 3 * order), jnp.float32),
            pltpu.VMEM((order, 3 * order), jnp.bfloat16),
            pltpu.VMEM((order, 3 * order), jnp.bfloat16),
        ],
    )(index, parts)


def slots(scaled, wanted, named, slot_count):
    place = jnp.cumsum(named.astype(jnp.int32)) - 1
    out = []
    for slot in range(slot_count):
        chosen = jnp.zeros(scaled.shape[1:], jnp.float32)
        for r in range(scaled.shape[0]):
            chosen = jnp.where(wanted[r] & (place[r] == slot), scaled[r], chosen)
        out.append(chosen)
    return jnp.concatenate(out, axis=0).astype(jnp.bfloat16)


def shards(design, process, prior_prec, routes, counts):
    row_count = process.shape[1]
    order = process.shape[2]
    my_time = lax.axis_index("tm")
    swath_index = lax.axis_index("swath")
    swath_size = lax.axis_size("swath")
    block_count = routes.shape[1]
    slot_count = block_count // 2
    block_rows = design.shape[1] // block_count
    total_slots = 2 * slot_count * block_rows * swath_size
    row_start = swath_index * row_count
    raw_rows = design[0].reshape(block_count, block_rows, order).astype(jnp.float32)
    mean_sq = jnp.mean(raw_rows * raw_rows, axis=-1, keepdims=True)
    scaled = raw_rows * lax.rsqrt(4.0 * total_slots * (mean_sq + 1e-06))
    live = jnp.arange(block_count) < counts[0, 0]
    target = routes[0]
    own, ahead = target == my_time, target == my_time + 1
    own_blocks = slots(scaled, live & own, own, slot_count)
    ahead_blocks = slots(scaled, live & ahead, ahead, slot_count)
    sent = jnp.concatenate([ahead_blocks, process[0]], axis=0)
    arrived = passed_along(sent, "tm", 1)
    prior = prior_prec[0]
    first = lax.reduce_precision(prior, 8, 7)
    second = lax.reduce_precision(prior - first, 8, 7)
    third = lax.reduce_precision(prior - first - second, 8, 7)
    pieces = jnp.zeros((16, order), jnp.float32)
    for i, piece in enumerate((first, second, third)):
        pieces = pieces.at[i, :row_count].set(piece)
    packed = jnp.concatenate(
        [own_blocks, arrived, process[0], pieces.astype(jnp.bfloat16)], axis=0
    )
    whole = lax.all_gather(packed, "swath", axis=0)
    observed = whole[:, : 2 * slot_count * block_rows].reshape(-1, order)
    cut = 2 * slot_count * block_rows
    previous = whole[:, cut : cut + row_count].reshape(order, order).astype(jnp.float32)
    cut += row_count
    current = whole[:, cut : cut + row_count].reshape(order, order).astype(jnp.float32)
    cut += row_count
    three = whole[:, cut : cut + 3, :row_count].astype(jnp.float32)
    prior_full = (three[:, 0] + three[:, 1] + three[:, 2]).reshape(order)
    gram = lax.dot_general(
        observed, observed, (((0,), (0,)), ((), ())), preferred_element_type=jnp.float32
    )
    full_diag = previous + current + gram + jnp.diag(prior_full)
    diag_rows = lax.dynamic_slice_in_dim(full_diag, row_start, row_count, 0)
    parts = jnp.stack(
        [m.reshape(swath_size, row_count, order) for m in (full_diag, current, previous.T)],
        axis=1,
    )
    index = swath_index.reshape(1).astype(jnp.int32)
    for level in range(LEVELS):
        distance = 2**level
        up, down = eliminate(index, parts)
        from_left = passed_along(up, "tm", distance)
        from_right = passed_along(down, "tm", -distance)
        diag_rows = diag_rows - from_left[:, :order] - from_right[:, order:]
        coup_rows = from_right[:, :order]
        if level < LEVELS - 1:
            mine = jnp.stack([diag_rows, coup_rows, from_left[:, order:]])
            parts = lax.all_gather(mine, "swath", axis=0)
    return (diag_rows[None], -coup_rows[None])


def solution(mesh):
    return jax.shard_map(
        shards,
        mesh=mesh,
        in_specs=(
            P("tm", "swath", None),
            P("tm", "swath", None),
            P("tm", "swath"),
            P("tm", "swath"),
            P("tm", "swath"),
        ),
        out_specs=(P("tm", "swath", None), P("tm", "swath", None)),
        check_vma=False,
    )
```

time: 783 us -> 383 us (0.49); the launches traced: 771 us -> 382 us
  other arithmetic: 488 us -> 13.9 us
  Pallas kernels: 0 us -> 156 us
  local copies, waits for them, and re-layouts: 62.4 us -> 3.7 us
  matrix products: 59.8 us -> 3.9 us
  waiting for transfers between devices: 103 us -> 149 us
  starting transfers between devices: 33.8 us -> 20.3 us
  between operations: 23.7 us -> 35 us
    another operation x64 -> x6, other arithmetic: 481 us -> 4.55 us  [the longest x1 2.2 us: shards(): jnp.stack([m.reshape(swath_size, row_count, order) for m in (full_diag, c...]
    pallas_call x0 -> x3, Pallas kernels: none -> 156 us  [eliminate(): pl.pallas_call(level_kernel, out_shape=(out, out), in_specs=[pl.BlockSpec...]
    another operation x91 -> x1, local copies, waits for them, and re-layouts: 48.9 us -> 0.34 us  [shards(): jnp.stack([m.reshape(swath_size, row_count, order) for m in (full_diag, c...]
    another operation x60 -> x0, matrix products: 36.1 us -> none  [the longest x42 30.5 us: tri_solve(): lax.linalg.triangular_solve(factor, right, left_side=True, lower=True)]
    all_gather x13 -> x3, waiting for transfers between devices: 63 us -> 86.3 us  [the longest x2 57 us: shards(): parts = lax.all_gather(mine, 'swath', axis=0)]
    ppermute x11 -> x7, waiting for transfers between devices: 40.1 us -> 63.1 us  [passed_along(): return lax.ppermute(block, axis, route)]
    dot_general x10 -> x1, matrix products: 23.7 us -> 3.9 us  [shards(): lax.dot_general(observed, observed, (((0,), (0,)), ((), ())), preferred_e...]
    ppermute x11 -> x7, starting transfers between devices: 32.3 us -> 20 us  [passed_along(): return lax.ppermute(block, axis, route)]
  transfers between devices with their start and end apart: 24 -> 10, of which waited for: 14 -> 8; matrix products, arithmetic and copies ran while one was open for 77% -> 0% of each run, Pallas kernels for 0% -> 0%
where the time goes in v1:
time: 383 us; the launch traced here: 382 us
  Pallas kernels  156 us (41%)
  waiting for transfers between devices  149 us (39%)
  between operations  35 us (9%)
  starting transfers between devices  20.3 us (5%)
  other arithmetic  13.9 us (4%)
  matrix products  3.9 us (1%)
    pallas_call x3, Pallas kernels, eliminate(): pl.pallas_call(level_kernel, out_shape=(out, out), in_specs=[pl.BlockSpec...  156 us
    ppermute x7, waiting for transfers between devices, passed_along(): return lax.ppermute(block, axis, route)  63.1 us
    all_gather x2, waiting for transfers between devices, shards(): parts = lax.all_gather(mine, 'swath', axis=0)  57 us
    all_gather x1, waiting for transfers between devices, shards(): whole = lax.all_gather(packed, 'swath', axis=0)  29.3 us
    ppermute x7, starting transfers between devices, passed_along(): return lax.ppermute(block, axis, route)  20 us
  transfers between devices with their start and end apart: 10, of which 8 were waited for; matrix products, arithmetic and copies ran while one was open for 0% of the time, Pallas kernels for 0%

profile of v1, /device:TPU:0, one launch (start us, length us, event | category | flops | bytes accessed | tf_op | source)
XLA Modules:
  0.0 382.0 jit_solution(15776342004945739250)
XLA Ops:
  8.1 0.7 fusion.23
  14.5 0.7 bitcast_and_fusion
  15.2 0.7 fusion.24
  20.8 1.2 multiply_reduce_fusion
  22.0 1.2 broadcast_multiply_fusion
  23.4 0.9 pad_maximum_fusion.3
  24.3 4.9 %collective-permute-start = (bf16[384,512]{1,0:T(8,128)(2,1)S(1)}, bf16[384,512]{1,0:T(8,128)(2,1)S(1)}, u32[]{:S(2)}, u32[]{:S(2)}) collective-permute-start(bf16[384,512]{1,0:T(8,128)(2,1)S(1)} %pad_maximum_fusion.3), channel_id=1, source_target_pairs={{0,4},{4,8},{8,12},{12,16},{16,20},{20,24},{24,28},{1,5},{5,9},{9,... | collective-permute-start | bytes 1179656 | tf_op jit(solution)/shard_map/ppermute | solution.py:16
  41.1 0.9 copy-done.1
  42.0 29.3 %all-gather.7.cloned.1.call-done = bf16[3136,512]{1,0:T(8,128)(2,1)} async-done(((bf16[784,512]{1,0:T(8,128)(2,1)}), bf16[3136,512]{1,0:T(8,128)(2,1)}) %all-gather.7.cloned.1.call-update) | async-done | bytes 3211280 | tf_op jit(solution)/shard_map/all_gather | solution.py:161
  71.3 2.5 slice_convert_fusion
  73.7 0.7 slice_convert_fusion.1
  75.1 3.9 %fusion.8 = f32[512,512]{1,0:T(8,128)S(1)} fusion(bf16[4,784,512]{2,1,0:T(8,128)(2,1)} %bitcast.109, f32[512,512]{1,0:T(8,128)} %bitcast.105, bf16[512,512]{1,0:T(8,128)(2,1)} %bitcast.102, f32[512]{0:T(512)S(1)} %bitcast.110), kind=kOutput, calls=%fused_computation.7 | convolution fusion | flops 1075314688 | bytes 4720640 | tf_op jit(solution)/shard_map/dot_general | solution.py:170
  79.0 2.2 pad_maximum_fusion.parts_ref
  81.2 51.9 %shard_map.68 = (f32[128,1024]{1,0:T(8,128)}, f32[128,1024]{1,0:T(8,128)}) custom-call(s32[1]{0:T(128)} %bitcast.49.index_ref, f32[4,3,128,512]{3,2,1,0:T(8,128)} %pad_maximum_fusion.parts_ref), custom_call_target="tpu_custom_call" | custom-call | tf_op jit(solution)/shard_map/pallas_call | solution.py:103
  133.1 3.4 collective-permute-start.1
  136.5 1.3 collective-permute-start.2
  137.8 21.8 %collective-permute-done.1 = f32[128,1024]{1,0:T(8,128)S(1)} collective-permute-done((f32[128,1024]{1,0:T(8,128)}, f32[128,1024]{1,0:T(8,128)S(1)}, u32[]{:S(2)}, u32[]{:S(2)}) %collective-permute-start.1) | collective-permute-done | bytes 524320 | tf_op jit(solution)/shard_map/ppermute | solution.py:16
  159.7 0.9 pad_maximum_fusion.1
  160.9 29.3 %all-gather.9.cloned.1.call-done = f32[12,128,512]{2,1,0:T(8,128)} async-done(((f32[3,128,512]{2,1,0:T(8,128)}), f32[12,128,512]{2,1,0:T(8,128)}) %all-gather.9.cloned.1.call-update) | async-done | bytes 3145744 | tf_op jit(solution)/shard_map/all_gather | solution.py:189
  190.2 51.9 %shard_map.69 = (f32[128,1024]{1,0:T(8,128)}, f32[128,1024]{1,0:T(8,128)}) custom-call(s32[1]{0:T(128)} %bitcast.49.index_ref, f32[4,3,128,512]{3,2,1,0:T(8,128)} %bitcast.100), custom_call_target="tpu_custom_call" | custom-call | tf_op jit(solution)/shard_map/pallas_call | solution.py:103
  242.1 3.4 collective-permute-start.3
  245.5 1.3 collective-permute-start.4
  246.8 10.6 %collective-permute-done.3 = f32[128,1024]{1,0:T(8,128)S(1)} collective-permute-done((f32[128,1024]{1,0:T(8,128)}, f32[128,1024]{1,0:T(8,128)S(1)}, u32[]{:S(2)}, u32[]{:S(2)}) %collective-permute-start.3) | collective-permute-done | bytes 524320 | tf_op jit(solution)/shard_map/ppermute | solution.py:16
  257.4 4.0 %collective-permute-done.4 = f32[128,1024]{1,0:T(8,128)S(1)} collective-permute-done((f32[128,1024]{1,0:T(8,128)}, f32[128,1024]{1,0:T(8,128)S(1)}, u32[]{:S(2)}, u32[]{:S(2)}) %collective-permute-start.4) | collective-permute-done | bytes 524320 | tf_op jit(solution)/shard_map/ppermute | solution.py:16
  261.5 0.9 pad_maximum_fusion.2
  262.5 27.7 %all-gather.11.cloned.1.call-done = f32[12,128,512]{2,1,0:T(8,128)} async-done(((f32[3,128,512]{2,1,0:T(8,128)}), f32[12,128,512]{2,1,0:T(8,128)}) %all-gather.11.cloned.1.call-update) | async-done | bytes 3145744 | tf_op jit(solution)/shard_map/all_gather | solution.py:189
  290.2 51.9 %shard_map.70 = (f32[128,1024]{1,0:T(8,128)}, f32[128,1024]{1,0:T(8,128)}) custom-call(s32[1]{0:T(128)} %bitcast.49.index_ref, f32[4,3,128,512]{3,2,1,0:T(8,128)} %bitcast.101), custom_call_target="tpu_custom_call" | custom-call | tf_op jit(solution)/shard_map/pallas_call | solution.py:103
  342.1 4.3 %collective-permute-start.5 = (f32[128,1024]{1,0:T(8,128)}, f32[128,1024]{1,0:T(8,128)S(1)}, u32[]{:S(2)}, u32[]{:S(2)}) collective-permute-start(f32[128,1024]{1,0:T(8,128)} %get-tuple-element.48), channel_id=1, source_target_pairs={{0,16},{4,20},{8,24},{12,28},{1,17},{5,21},{9,25},{13,29},{2,18},{... | collective-permute-start | bytes 1572872 | tf_op jit(solution)/shard_map/ppermute | solution.py:16
  346.5 1.3 collective-permute-start.6
  347.8 10.6 %collective-permute-done.5 = f32[128,1024]{1,0:T(8,128)S(1)} collective-permute-done((f32[128,1024]{1,0:T(8,128)}, f32[128,1024]{1,0:T(8,128)S(1)}, u32[]{:S(2)}, u32[]{:S(2)}) %collective-permute-start.5) | collective-permute-done | bytes 524320 | tf_op jit(solution)/shard_map/ppermute | solution.py:16
  358.4 16.1 %collective-permute-done.6 = f32[128,1024]{1,0:T(8,128)S(1)} collective-permute-done((f32[128,1024]{1,0:T(8,128)}, f32[128,1024]{1,0:T(8,128)S(1)}, u32[]{:S(2)}, u32[]{:S(2)}) %collective-permute-start.6) | collective-permute-done | bytes 524320 | tf_op jit(solution)/shard_map/ppermute | solution.py:16
  374.5 0.9 fusion.11
  (37 shorter events, 3.5 us)
Async XLA Ops:
  7.2 33.9 %copy-start.2 = (bf16[1,128,512]{2,1,0:T(8,128)(2,1)S(1)}, bf16[1,128,512]{2,1,0:T(8,128)(2,1)}, u32[]{:S(2)}) copy-start(bf16[1,128,512]{2,1,0:T(8,128)(2,1)} %param.12) | copy-start | bytes 393220
  7.2 33.2 %copy-start.3 = (f32[1,128]{1,0:T(1,128)S(1)}, f32[1,128]{1,0:T(1,128)}, u32[]{:S(2)}) copy-start(f32[1,128]{1,0:T(1,128)} %param.13) | copy-start | bytes 1540
  7.2 64.1 %all-gather.7.cloned.1.call-start = ((), (), s32[]{:S(2)}) async-start(), calls=%async_computation | async-start | bytes 4014080 | tf_op jit(solution)/shard_map/all_gather | solution.py:161
  24.3 16.6 %collective-permute-start = (bf16[384,512]{1,0:T(8,128)(2,1)S(1)}, bf16[384,512]{1,0:T(8,128)(2,1)S(1)}, u32[]{:S(2)}, u32[]{:S(2)}) collective-permute-start(bf16[384,512]{1,0:T(8,128)(2,1)S(1)} %pad_maximum_fusion.3), channel_id=1, source_target_pairs={{0,4},{4,8},{8,12},{12,16},{16,20},{20,24},{24,28},{1,5},{5,9},{9,... | collective-permute-start | bytes 1179656 | tf_op jit(solution)/shard_map/ppermute | solution.py:16
  41.1 0.9 copy-start.1
  42.0 148.2 %all-gather.9.cloned.1.call-start = ((), (), s32[]{:S(2)}) async-start(), calls=%async_computation.1 | async-start | bytes 3932160 | tf_op jit(solution)/shard_map/all_gather | solution.py:189
  73.7 0.8 copy-start
  133.1 26.5 %collective-permute-start.1 = (f32[128,1024]{1,0:T(8,128)}, f32[128,1024]{1,0:T(8,128)S(1)}, u32[]{:S(2)}, u32[]{:S(2)}) collective-permute-start(f32[128,1024]{1,0:T(8,128)} %get-tuple-element.44), channel_id=1, source_target_pairs={{0,4},{4,8},{8,12},{12,16},{16,20},{20,24},{24,28},{1,5},{5,9},{9,... | collective-permute-start | bytes 1572872 | tf_op jit(solution)/shard_map/ppermute | solution.py:16
  136.5 23.1 %collective-permute-start.2 = (f32[128,1024]{1,0:T(8,128)}, f32[128,1024]{1,0:T(8,128)S(1)}, u32[]{:S(2)}, u32[]{:S(2)}) collective-permute-start(f32[128,1024]{1,0:T(8,128)} %get-tuple-element.45), channel_id=1, source_target_pairs={{4,0},{8,4},{12,8},{16,12},{20,16},{24,20},{28,24},{5,1},{9,5},{13... | collective-permute-start | bytes 1572872 | tf_op jit(solution)/shard_map/ppermute | solution.py:16
  160.7 129.6 %all-gather.11.cloned.1.call-start = ((), (), s32[]{:S(2)}) async-start(), calls=%async_computation.2 | async-start | bytes 3932160 | tf_op jit(solution)/shard_map/all_gather | solution.py:189
  242.1 15.3 %collective-permute-start.3 = (f32[128,1024]{1,0:T(8,128)}, f32[128,1024]{1,0:T(8,128)S(1)}, u32[]{:S(2)}, u32[]{:S(2)}) collective-permute-start(f32[128,1024]{1,0:T(8,128)} %get-tuple-element.46), channel_id=1, source_target_pairs={{0,8},{4,12},{8,16},{12,20},{16,24},{20,28},{1,9},{5,13},{9,17},{1... | collective-permute-start | bytes 1572872 | tf_op jit(solution)/shard_map/ppermute | solution.py:16
  245.5 15.9 %collective-permute-start.4 = (f32[128,1024]{1,0:T(8,128)}, f32[128,1024]{1,0:T(8,128)S(1)}, u32[]{:S(2)}, u32[]{:S(2)}) collective-permute-start(f32[128,1024]{1,0:T(8,128)} %get-tuple-element.47), channel_id=1, source_target_pairs={{8,0},{12,4},{16,8},{20,12},{24,16},{28,20},{9,1},{13,5},{17,9},{2... | collective-permute-start | bytes 1572872 | tf_op jit(solution)/shard_map/ppermute | solution.py:16
  342.1 16.2 %collective-permute-start.5 = (f32[128,1024]{1,0:T(8,128)}, f32[128,1024]{1,0:T(8,128)S(1)}, u32[]{:S(2)}, u32[]{:S(2)}) collective-permute-start(f32[128,1024]{1,0:T(8,128)} %get-tuple-element.48), channel_id=1, source_target_pairs={{0,16},{4,20},{8,24},{12,28},{1,17},{5,21},{9,25},{13,29},{2,18},{... | collective-permute-start | bytes 1572872 | tf_op jit(solution)/shard_map/ppermute | solution.py:16
  346.5 28.0 %collective-permute-start.6 = (f32[128,1024]{1,0:T(8,128)}, f32[128,1024]{1,0:T(8,128)S(1)}, u32[]{:S(2)}, u32[]{:S(2)}) collective-permute-start(f32[128,1024]{1,0:T(8,128)} %get-tuple-element.49), channel_id=1, source_target_pairs={{16,0},{20,4},{24,8},{28,12},{17,1},{21,5},{25,9},{29,13},{18,2},{... | collective-permute-start | bytes 1572872 | tf_op jit(solution)/shard_map/ppermute | solution.py:16
Sparse Core Ops, SparseCore 0:
  42.1 29.1 all-gather.6
  160.8 29.3 all-gather.8
  262.6 27.5 all-gather.10

commit v2 on v1

v2 whole, which is shorter than its diff:
```python
import functools

import jax
import jax.numpy as jnp
from jax import lax
from jax.experimental import pallas as pl
from jax.experimental.pallas import tpu as pltpu
from jax.sharding import PartitionSpec as P

LEVELS = 3


def passed_along(block, axis, distance):
    devices = range(lax.axis_size(axis))
    route = [(i - distance, i) for i in devices if i - distance in devices]
    return lax.ppermute(block, axis, route)


def split(x):
    high = x.astype(jnp.bfloat16)
    return high, (x - high.astype(jnp.float32)).astype(jnp.bfloat16)


def dot3(a, b, left):
    (ah, al), (bh, bl) = a, b
    dot = functools.partial(
        lax.dot_general,
        dimension_numbers=(((left,), (0,)), ((), ())),
        preferred_element_type=jnp.float32,
    )
    return dot(ah, bh) + (dot(ah, bl) + dot(al, bh))


def factor_inverse(m, width=8):
    n = m.shape[0]
    groups = n // width
    rows = [m[width * g : width * (g + 1), :] for g in range(groups)]
    lane = lax.broadcasted_iota(jnp.int32, (width, n), 1)
    sub = lax.broadcasted_iota(jnp.int32, (width, n), 0)
    spread = lambda x: jnp.broadcast_to(x, (width, n))
    for g in range(groups):
        first = width * g
        inside = (lane >= first) & (lane < first + width)
        columns = {
            h: [spread(rows[h][:, first + s : first + s + 1]) for s in range(width)]
            for h in range(g, groups)
        }
        entry = {
            (k, s): spread(columns[g][s][k : k + 1, :])
            for s in range(width)
            for k in range(s, width)
        }
        solved = [
            jnp.where(lane == first + s, 1.0, jnp.where(inside, 0.0, spread(rows[g][s : s + 1, :])))
            for s in range(width)
        ]
        scale, lower = [], {}
        for s in range(width):
            scale.append(lax.rsqrt(entry[s, s]))
            solved[s] = solved[s] * scale[s]
            for k in range(s + 1, width):
                lower[k, s] = entry[k, s] * scale[s]
            for k in range(s + 1, width):
                for t in range(s + 1, k + 1):
                    entry[k, t] = entry[k, t] - lower[k, s] * lower[t, s]
                solved[k] = solved[k] - lower[k, s] * solved[s]
        back = list(solved)
        for s in range(width - 1, -1, -1):
            back[s] = back[s] * scale[s]
            for k in range(s):
                back[k] = back[k] - lower[s, k] * back[s]
        for h in range(g + 1, groups):
            left = jnp.where(inside, 0.0, rows[h])
            for s in range(width):
                left = left - columns[h][s] * back[s]
            rows[h] = left
        group = solved[0]
        for s in range(1, width):
            group = jnp.where(sub == s, solved[s], group)
        rows[g] = group
    out = jnp.concatenate(rows, axis=0)
    down = lax.broadcasted_iota(jnp.int32, (n, n), 0)
    across = lax.broadcasted_iota(jnp.int32, (n, n), 1)
    return jnp.where(down >= across, out, 0.0)


def factor_kernel(diag_ref, high, low, work):
    blocks, rows, order = diag_ref.shape
    work[...] = diag_ref[...]
    for i in range(blocks):
        for k in range(i, blocks):
            here = work[i, :, k * rows : (k + 1) * rows]
            there = work[k, :, i * rows : (i + 1) * rows]
            work[i, :, k * rows : (k + 1) * rows] = 0.5 * (here + there.T)
    down = lax.broadcasted_iota(jnp.int32, (rows, rows), 0)
    across = lax.broadcasted_iota(jnp.int32, (rows, rows), 1)
    unit = jnp.where(down == across, 1.0, 0.0)
    column_block = lax.broadcasted_iota(jnp.int32, (rows, order), 1) // rows

    def step(j, carry):
        at = pl.ds(pl.multiple_of(j * rows, rows), rows)
        inverse = factor_inverse(work[j, :, at])
        work[j, :, at] = unit
        solved = dot3(split(inverse), split(work[j]), 1)
        solved_high, solved_low = split(solved)
        high[at, :] = solved_high
        low[at, :] = solved_low
        for i in range(1, blocks):

            @pl.when(i > j)
            def _():
                cut = slice(i * rows, (i + 1) * rows)
                left = (high[at, cut], low[at, cut])
                work[i, :, at] = jnp.zeros((rows, rows), jnp.float32)
                work[i] = work[i] - dot3(left, (solved_high, solved_low), 0)

        keep = column_block <= j
        high[at, :] = jnp.where(keep, solved_high, 0.0).astype(jnp.bfloat16)
        low[at, :] = jnp.where(keep, solved_low, 0.0).astype(jnp.bfloat16)
        return carry

    lax.fori_loop(0, blocks, step, 0)


def factor(diag):
    blocks, rows, order = diag.shape
    out = jax.ShapeDtypeStruct((order, order), jnp.bfloat16)
    return pl.pallas_call(
        factor_kernel,
        out_shape=(out, out),
        in_specs=[pl.BlockSpec(memory_space=pltpu.VMEM)],
        out_specs=(pl.BlockSpec(memory_space=pltpu.VMEM),) * 2,
        scratch_shapes=[pltpu.VMEM((blocks, rows, order), jnp.float32)],
        cost_estimate=pl.CostEstimate(flops=20000000000, bytes_accessed=4 * order * order, transcendentals=0),
    )(diag)


def term_kernel(index_ref, inverse_high, inverse_low, parts_ref, out_ref, high, low):
    blocks, _, rows, order = parts_ref.shape
    for part in range(2):
        across = slice(part * order, (part + 1) * order)
        right = [split(parts_ref[i, part]) for i in range(blocks)]
        right = [jnp.concatenate([r[k] for r in right], axis=0) for k in range(2)]
        for j in range(blocks):
            at, deep = slice(j * rows, (j + 1) * rows), (j + 1) * rows
            left = (inverse_high[at, :deep], inverse_low[at, :deep])
            solved = dot3(left, (right[0][:deep], right[1][:deep]), 1)
            solved_high, solved_low = split(solved)
            high[at, across] = solved_high
            low[at, across] = solved_low
    mine = index_ref[0] * rows
    for k, (first, second) in enumerate(((0, 0), (0, 1), (1, 1), (1, 0))):
        cut = pl.ds(pl.multiple_of(first * order + mine, rows), rows)
        across = slice(second * order, (second + 1) * order)
        out_ref[k] = dot3((high[:, cut], low[:, cut]), (high[:, across], low[:, across]), 0)


def terms(index, inverse, parts):
    blocks, _, rows, order = parts.shape
    return pl.pallas_call(
        term_kernel,
        out_shape=jax.ShapeDtypeStruct((4, rows, order), jnp.float32),
        in_specs=[pl.BlockSpec(memory_space=pltpu.SMEM)]
        + [pl.BlockSpec(memory_space=pltpu.VMEM)] * 3,
        out_specs=pl.BlockSpec(memory_space=pltpu.VMEM),
        scratch_shapes=[pltpu.VMEM((order, 2 * order), jnp.bfloat16)] * 2,
        cost_estimate=pl.CostEstimate(flops=4000000000, bytes_accessed=16 * order * order, transcendentals=0),
    )(index, *inverse, parts)


def slots(scaled, wanted, named, slot_count):
    place = jnp.cumsum(named.astype(jnp.int32)) - 1
    out = []
    for slot in range(slot_count):
        chosen = jnp.zeros(scaled.shape[1:], jnp.float32)
        for r in range(scaled.shape[0]):
            chosen = jnp.where(wanted[r] & (place[r] == slot), scaled[r], chosen)
        out.append(chosen)
    return jnp.concatenate(out, axis=0).astype(jnp.bfloat16)


def shards(design, process, prior_prec, routes, counts):
    row_count = process.shape[1]
    order = process.shape[2]
    my_time = lax.axis_index("tm")
    swath_index = lax.axis_index("swath")
    swath_size = lax.axis_size("swath")
    block_count = routes.shape[1]
    slot_count = block_count // 2
    block_rows = design.shape[1] // block_count
    total_slots = 2 * slot_count * block_rows * swath_size
    row_start = swath_index * row_count
    raw_rows = design[0].reshape(block_count, block_rows, order).astype(jnp.float32)
    mean_sq = jnp.mean(raw_rows * raw_rows, axis=-1, keepdims=True)
    scaled = raw_rows * lax.rsqrt(4.0 * total_slots * (mean_sq + 1e-06))
    live = jnp.arange(block_count) < counts[0, 0]
    target = routes[0]
    own, ahead = target == my_time, target == my_time + 1
    own_blocks = slots(scaled, live & own, own, slot_count)
    ahead_blocks = slots(scaled, live & ahead, ahead, slot_count)
    sent = jnp.concatenate([ahead_blocks, process[0]], axis=0)
    arrived = passed_along(sent, "tm", 1)
    prior = prior_prec[0]
    first = lax.reduce_precision(prior, 8, 7)
    second = lax.reduce_precision(prior - first, 8, 7)
    third = lax.reduce_precision(prior - first - second, 8, 7)
    pieces = jnp.zeros((16, order), jnp.float32)
    for i, piece in enumerate((first, second, third)):
        pieces = pieces.at[i, :row_count].set(piece)
    near = jnp.concatenate([own_blocks, process[0], pieces.astype(jnp.bfloat16)], axis=0)
    near = lax.all_gather(near, "swath", axis=0)
    far = lax.all_gather(arrived, "swath", axis=0)
    cut = slot_count * block_rows
    over_rows = lambda w: lax.dot_general(
        w, w, (((0,), (0,)), ((), ())), preferred_element_type=jnp.float32
    )
    previous = far[:, cut:].reshape(order, order).astype(jnp.float32)
    current = near[:, cut : cut + row_count].reshape(order, order).astype(jnp.float32)
    three = near[:, cut + row_count : cut + row_count + 3, :row_count].astype(jnp.float32)
    prior_full = (three[:, 0] + three[:, 1] + three[:, 2]).reshape(order)
    gram = over_rows(near[:, :cut].reshape(-1, order)) + over_rows(far[:, :cut].reshape(-1, order))
    full_diag = previous + current + gram + jnp.diag(prior_full)
    diag_rows = lax.dynamic_slice_in_dim(full_diag, row_start, row_count, 0)
    full_diag = full_diag.reshape(swath_size, row_count, order)
    parts = jnp.stack(
        [m.reshape(swath_size, row_count, order) for m in (current, previous.T)], axis=1
    )
    index = swath_index.reshape(1).astype(jnp.int32)
    for level in range(LEVELS):
        distance = 2**level
        out = terms(index, factor(full_diag), parts)
        left_term = passed_along(out[0], "tm", distance)
        right_term = passed_along(out[2], "tm", -distance)
        diag_rows = diag_rows - left_term - right_term
        if level < LEVELS - 1:
            diag_rows, across, back = lax.optimization_barrier((diag_rows, out[1], out[3]))
            full_diag = lax.all_gather(diag_rows, "swath", axis=0)
            ahead = passed_along(across, "tm", distance)
            coup_rows = passed_along(back, "tm", -distance)
            full_diag, ahead, coup_rows = lax.optimization_barrier((full_diag, ahead, coup_rows))
            parts = lax.all_gather(jnp.stack([coup_rows, ahead]), "swath", axis=0)
        else:
            coup_rows = passed_along(out[3], "tm", -distance)
    return (diag_rows[None], -coup_rows[None])


def solution(mesh):
    return jax.shard_map(
        shards,
        mesh=mesh,
        in_specs=(
            P("tm", "swath", None),
            P("tm", "swath", None),
            P("tm", "swath"),
            P("tm", "swath"),
            P("tm", "swath"),
        ),
        out_specs=(P("tm", "swath", None), P("tm", "swath", None)),
        check_vma=False,
    )
```

time: 383 us -> 274 us (0.72)
  Pallas kernels: 156 us -> 89 us
  waiting for transfers between devices: 149 us -> 83.1 us
  starting transfers between devices: 20.3 us -> 36.7 us
  local copies, waits for them, and re-layouts: 3.7 us -> 8.87 us
    pallas_call x3 -> x6, Pallas kernels: 156 us -> 89 us  [the longest x3 72.7 us: factor(): pl.pallas_call(factor_kernel, out_shape=(out, out), in_specs=[pl.BlockSpe...]
    all_gather x3 -> x6, waiting for transfers between devices: 86.3 us -> 22.3 us  [the longest x1 16.6 us: shards(): far = lax.all_gather(arrived, 'swath', axis=0)]
    ppermute x7 -> x12, starting transfers between devices: 20 us -> 36.3 us  [passed_along(): return lax.ppermute(block, axis, route)]
    ppermute x7 -> x12, waiting for transfers between devices: 63.1 us -> 60.6 us  [passed_along(): return lax.ppermute(block, axis, route)]
  transfers between devices with their start and end apart: 10 -> 18, of which waited for: 8 -> 13; matrix products, arithmetic and copies ran while one was open for 0% -> 3% of each run, Pallas kernels for 0% -> 18%
where the time goes in v2:
time: 274 us; the launch traced here: 273 us
  Pallas kernels  89 us (32%)
  waiting for transfers between devices  83.1 us (30%)
  starting transfers between devices  36.7 us (13%)
  between operations  35 us (13%)
  other arithmetic  15.3 us (6%)
  local copies, waits for them, and re-layouts  8.87 us (3%)
  matrix products  5.05 us (2%)
    pallas_call x3, Pallas kernels, factor(): pl.pallas_call(factor_kernel, out_shape=(out, out), in_specs=[pl.BlockSpe...  72.7 us
    ppermute x12, waiting for transfers between devices, passed_along(): return lax.ppermute(block, axis, route)  60.6 us
    ppermute x12, starting transfers between devices, passed_along(): return lax.ppermute(block, axis, route)  36.3 us
    all_gather x1, waiting for transfers between devices, shards(): far = lax.all_gather(arrived, 'swath', axis=0)  16.6 us
    pallas_call x3, Pallas kernels, terms(): pl.pallas_call(term_kernel, out_shape=jax.ShapeDtypeStruct((4, rows, orde...  16.3 us
    all_gather x2, waiting for transfers between devices, shards(): full_diag = lax.all_gather(diag_rows, 'swath', axis=0)  5.68 us
  transfers between devices with their start and end apart: 18, of which 13 were waited for; matrix products, arithmetic and copies ran while one was open for 3% of the time, Pallas kernels for 18%

profile of v2, /device:TPU:0, one launch (start us, length us, event | category | flops | bytes accessed | tf_op | source)
XLA Modules:
  0.0 273.0 jit_solution(14884793561704080007)
XLA Ops:
  36.2 4.9 %collective-permute-start = (bf16[384,512]{1,0:T(8,128)(2,1)S(1)}, bf16[384,512]{1,0:T(8,128)(2,1)S(1)}, u32[]{:S(2)}, u32[]{:S(2)}) collective-permute-start(bf16[384,512]{1,0:T(8,128)(2,1)S(1)} %pad_maximum_fusion.4), channel_id=1, source_target_pairs={{0,4},{4,8},{8,12},{12,16},{16,20},{20,24},{24,28},{1,5},{5,9},{9,... | collective-permute-start | bytes 1179656 | tf_op jit(solution)/shard_map/ppermute | solution.py:16
  41.2 8.3 %collective-permute-done = bf16[384,512]{1,0:T(8,128)(2,1)S(1)} collective-permute-done((bf16[384,512]{1,0:T(8,128)(2,1)S(1)}, bf16[384,512]{1,0:T(8,128)(2,1)S(1)}, u32[]{:S(2)}, u32[]{:S(2)}) %collective-permute-start) | collective-permute-done | bytes 393248 | tf_op jit(solution)/shard_map/ppermute | solution.py:16
  51.1 3.3 %convolution_bitcast_fusion.1 = f32[512,512]{1,0:T(8,128)} fusion(bf16[4,400,512]{2,1,0:T(8,128)(2,1)} %bitcast.124), kind=kOutput, calls=%fused_computation.2 | convolution fusion | flops 536870912 | bytes 2097152 | tf_op jit(solution)/shard_map/dot_general | solution.py:214
  55.6 16.6 %all-gather.13.cloned.1.call-done = bf16[1536,512]{1,0:T(8,128)(2,1)} async-done(((bf16[384,512]{1,0:T(8,128)(2,1)}), bf16[1536,512]{1,0:T(8,128)(2,1)}) %all-gather.13.cloned.1.call-update) | async-done | bytes 1572880 | tf_op jit(solution)/shard_map/all_gather | solution.py:212
  74.1 1.8 fusion.2
  75.9 24.2 %shard_map.68 = (bf16[512,512]{1,0:T(8,128)(2,1)}, bf16[512,512]{1,0:T(8,128)(2,1)}) custom-call(f32[4,128,512]{2,1,0:T(8,128)} %bitcast.126), custom_call_target="tpu_custom_call" | custom-call | flops 20000000000 | bytes 1048576 | tf_op jit(solution)/shard_map/pallas_call | solution.py:128
  100.5 1.7 pad_maximum_fusion.parts_ref
  102.2 5.4 %shard_map.69 = f32[4,128,512]{2,1,0:T(8,128)} custom-call(s32[1]{0:T(128)} %bitcast.51.index_ref, bf16[512,512]{1,0:T(8,128)(2,1)} %get-tuple-element.56.inverse_high, bf16[512,512]{1,0:T(8,128)(2,1)} %get-tuple-element.57.inverse_low, f32[4,2,128,512]{3,2,1,0:T(8,128)} %pad_maximum_fusion.parts_ref), custom_call_target="tpu_custom_call" | custom-call | flops 4000000000 | bytes 4194304 | tf_op jit(solution)/shard_map/pallas_call | solution.py:160
  108.8 1.3 collective-permute-start.2
  110.1 4.6 %collective-permute-start.1 = (f32[128,512]{1,0:T(8,128)S(1)}, f32[128,512]{1,0:T(8,128)S(1)}, u32[]{:S(2)}, u32[]{:S(2)}) collective-permute-start(f32[128,512]{1,0:T(8,128)S(1)} %get-tuple-element.86), channel_id=1, source_target_pairs={{0,4},{4,8},{8,12},{12,16},{16,20},{20,24},{24,28},{1,5},{5,9},{9,... | collective-permute-start | bytes 786440 | tf_op jit(solution)/shard_map/ppermute | solution.py:16
  114.7 4.5 %collective-permute-done.2 = f32[128,512]{1,0:T(8,128)S(1)} collective-permute-done((f32[128,512]{1,0:T(8,128)S(1)}, f32[128,512]{1,0:T(8,128)S(1)}, u32[]{:S(2)}, u32[]{:S(2)}) %collective-permute-start.2) | collective-permute-done | bytes 262176 | tf_op jit(solution)/shard_map/ppermute | solution.py:16
  119.2 5.5 %collective-permute-done.1 = f32[128,512]{1,0:T(8,128)S(1)} collective-permute-done((f32[128,512]{1,0:T(8,128)S(1)}, f32[128,512]{1,0:T(8,128)S(1)}, u32[]{:S(2)}, u32[]{:S(2)}) %collective-permute-start.1) | collective-permute-done | bytes 262176 | tf_op jit(solution)/shard_map/ppermute | solution.py:16
  124.7 1.7 subtract_subtract_fusion.1
  126.5 4.4 %collective-permute-start.3 = (f32[128,512]{1,0:T(8,128)S(1)}, f32[128,512]{1,0:T(8,128)S(1)}, u32[]{:S(2)}, u32[]{:S(2)}) collective-permute-start(f32[128,512]{1,0:T(8,128)S(1)} %get-tuple-element.59), channel_id=1, source_target_pairs={{0,4},{4,8},{8,12},{12,16},{16,20},{20,24},{24,28},{1,5},{5,9},{9,... | collective-permute-start | bytes 786440 | tf_op jit(solution)/shard_map/ppermute | solution.py:16
  132.2 10.0 %collective-permute-done.3 = f32[128,512]{1,0:T(8,128)S(1)} collective-permute-done((f32[128,512]{1,0:T(8,128)S(1)}, f32[128,512]{1,0:T(8,128)S(1)}, u32[]{:S(2)}, u32[]{:S(2)}) %collective-permute-start.3) | collective-permute-done | bytes 262176 | tf_op jit(solution)/shard_map/ppermute | solution.py:16
  144.5 24.2 %shard_map.70 = (bf16[512,512]{1,0:T(8,128)(2,1)}, bf16[512,512]{1,0:T(8,128)(2,1)}) custom-call(f32[4,128,512]{2,1,0:T(8,128)} %bitcast.130), custom_call_target="tpu_custom_call" | custom-call | flops 20000000000 | bytes 1048576 | tf_op jit(solution)/shard_map/pallas_call | solution.py:128
  168.7 5.4 %shard_map.71 = f32[4,128,512]{2,1,0:T(8,128)} custom-call(s32[1]{0:T(128)} %bitcast.51.index_ref, bf16[512,512]{1,0:T(8,128)(2,1)} %get-tuple-element.62.inverse_high, bf16[512,512]{1,0:T(8,128)(2,1)} %get-tuple-element.63.inverse_low, f32[4,2,128,512]{3,2,1,0:T(8,128)} %bitcast.128), custom_call_target="tpu_custom_call" | custom-call | flops 4000000000 | bytes 4194304 | tf_op jit(solution)/shard_map/pallas_call | solution.py:160
  174.1 1.3 slice_bitcast_fusion.3
  176.7 4.6 %collective-permute-start.5 = (f32[128,512]{1,0:T(8,128)S(1)}, f32[128,512]{1,0:T(8,128)S(1)}, u32[]{:S(2)}, u32[]{:S(2)}) collective-permute-start(f32[128,512]{1,0:T(8,128)S(1)} %get-tuple-element.82), channel_id=1, source_target_pairs={{0,8},{4,12},{8,16},{12,20},{16,24},{20,28},{1,9},{5,13},{9,17},{1... | collective-permute-start | bytes 786440 | tf_op jit(solution)/shard_map/ppermute | solution.py:16
  181.3 4.5 %collective-permute-done.6 = f32[128,512]{1,0:T(8,128)S(1)} collective-permute-done((f32[128,512]{1,0:T(8,128)S(1)}, f32[128,512]{1,0:T(8,128)S(1)}, u32[]{:S(2)}, u32[]{:S(2)}) %collective-permute-start.6) | collective-permute-done | bytes 262176 | tf_op jit(solution)/shard_map/ppermute | solution.py:16
  187.8 4.4 %collective-permute-start.7 = (f32[128,512]{1,0:T(8,128)S(1)}, f32[128,512]{1,0:T(8,128)S(1)}, u32[]{:S(2)}, u32[]{:S(2)}) collective-permute-start(f32[128,512]{1,0:T(8,128)S(1)} %get-tuple-element.67), channel_id=1, source_target_pairs={{0,8},{4,12},{8,16},{12,20},{16,24},{20,28},{1,9},{5,13},{9,17},{1... | collective-permute-start | bytes 786440 | tf_op jit(solution)/shard_map/ppermute | solution.py:16
  192.2 1.5 collective-permute-start.8
  193.7 3.3 %collective-permute-done.7 = f32[128,512]{1,0:T(8,128)S(1)} collective-permute-done((f32[128,512]{1,0:T(8,128)S(1)}, f32[128,512]{1,0:T(8,128)S(1)}, u32[]{:S(2)}, u32[]{:S(2)}) %collective-permute-start.7) | collective-permute-done | bytes 262176 | tf_op jit(solution)/shard_map/ppermute | solution.py:16
  197.0 4.1 %collective-permute-done.8 = f32[128,512]{1,0:T(8,128)S(1)} collective-permute-done((f32[128,512]{1,0:T(8,128)S(1)}, f32[128,512]{1,0:T(8,128)S(1)}, u32[]{:S(2)}, u32[]{:S(2)}) %collective-permute-start.8) | collective-permute-done | bytes 262176 | tf_op jit(solution)/shard_map/ppermute | solution.py:16
  201.1 4.5 %all-gather.21.cloned.1.call-done = f32[512,512]{1,0:T(8,128)} async-done(((f32[128,512]{1,0:T(8,128)}), f32[512,512]{1,0:T(8,128)}) %all-gather.21.cloned.1.call-update) | async-done | bytes 1048592 | tf_op jit(solution)/shard_map/all_gather | solution.py:237
  206.5 24.2 %shard_map.72 = (bf16[512,512]{1,0:T(8,128)(2,1)}, bf16[512,512]{1,0:T(8,128)(2,1)}) custom-call(f32[4,128,512]{2,1,0:T(8,128)} %bitcast.131), custom_call_target="tpu_custom_call" | custom-call | flops 20000000000 | bytes 1048576 | tf_op jit(solution)/shard_map/pallas_call | solution.py:128
  230.7 5.4 %shard_map.73 = f32[4,128,512]{2,1,0:T(8,128)} custom-call(s32[1]{0:T(128)} %bitcast.51.index_ref, bf16[512,512]{1,0:T(8,128)(2,1)} %get-tuple-element.70.inverse_high, bf16[512,512]{1,0:T(8,128)(2,1)} %get-tuple-element.71.inverse_low, f32[4,2,128,512]{3,2,1,0:T(8,128)} %bitcast.129), custom_call_target="tpu_custom_call" | custom-call | flops 4000000000 | bytes 4194304 | tf_op jit(solution)/shard_map/pallas_call | solution.py:160
  237.3 1.3 collective-permute-start.11
  238.6 1.3 collective-permute-start.10
  239.9 5.5 %collective-permute-start.9 = (f32[128,512]{1,0:T(8,128)S(1)}, f32[128,512]{1,0:T(8,128)S(1)}, u32[]{:S(2)}, u32[]{:S(2)}) collective-permute-start(f32[128,512]{1,0:T(8,128)S(1)} %get-tuple-element.78), channel_id=1, source_target_pairs={{0,16},{4,20},{8,24},{12,28},{1,17},{5,21},{9,25},{13,29},{2,18},{... | collective-permute-start | bytes 786440 | tf_op jit(solution)/shard_map/ppermute | solution.py:16
  245.4 15.1 %collective-permute-done.11 = f32[128,512]{1,0:T(8,128)S(1)} collective-permute-done((f32[128,512]{1,0:T(8,128)S(1)}, f32[128,512]{1,0:T(8,128)S(1)}, u32[]{:S(2)}, u32[]{:S(2)}) %collective-permute-start.11) | collective-permute-done | bytes 262176 | tf_op jit(solution)/shard_map/ppermute | solution.py:16
  261.3 4.1 %collective-permute-done.10 = f32[128,512]{1,0:T(8,128)S(1)} collective-permute-done((f32[128,512]{1,0:T(8,128)S(1)}, f32[128,512]{1,0:T(8,128)S(1)}, u32[]{:S(2)}, u32[]{:S(2)}) %collective-permute-start.10) | collective-permute-done | bytes 262176 | tf_op jit(solution)/shard_map/ppermute | solution.py:16
  (66 shorter events, 25.0 us)
Async XLA Ops:
  7.2 17.3 %copy-start.2 = (bf16[1,128,512]{2,1,0:T(8,128)(2,1)S(1)}, bf16[1,128,512]{2,1,0:T(8,128)(2,1)}, u32[]{:S(2)}) copy-start(bf16[1,128,512]{2,1,0:T(8,128)(2,1)} %param.12) | copy-start | bytes 393220
  7.2 43.2 %all-gather.15.cloned.1.call-start = ((), (), s32[]{:S(2)}) async-start(), calls=%async_computation.1 | async-start | bytes 2048000 | tf_op jit(solution)/shard_map/all_gather | solution.py:211
  25.3 47.0 %all-gather.13.cloned.1.call-start = ((), (), s32[]{:S(2)}) async-start(), calls=%async_computation | async-start | bytes 1966080 | tf_op jit(solution)/shard_map/all_gather | solution.py:212
  36.2 13.3 %collective-permute-start = (bf16[384,512]{1,0:T(8,128)(2,1)S(1)}, bf16[384,512]{1,0:T(8,128)(2,1)S(1)}, u32[]{:S(2)}, u32[]{:S(2)}) collective-permute-start(bf16[384,512]{1,0:T(8,128)(2,1)S(1)} %pad_maximum_fusion.4), channel_id=1, source_target_pairs={{0,4},{4,8},{8,12},{12,16},{16,20},{20,24},{24,28},{1,5},{5,9},{9,... | collective-permute-start | bytes 1179656 | tf_op jit(solution)/shard_map/ppermute | solution.py:16
  49.5 0.8 copy-start.3
  50.3 93.1 %all-gather.17.cloned.1.call-start = ((), (), s32[]{:S(2)}) async-start(), calls=%async_computation.2 | async-start | bytes 1310720 | tf_op jit(solution)/shard_map/all_gather | solution.py:237
  72.3 1.6 copy-start.4
  72.3 1.9 copy-start.5
  108.8 10.3 %collective-permute-start.2 = (f32[128,512]{1,0:T(8,128)S(1)}, f32[128,512]{1,0:T(8,128)S(1)}, u32[]{:S(2)}, u32[]{:S(2)}) collective-permute-start(f32[128,512]{1,0:T(8,128)S(1)} %get-tuple-element.85), channel_id=1, source_target_pairs={{4,0},{8,4},{12,8},{16,12},{20,16},{24,20},{28,24},{5,1},{9,5},{13... | collective-permute-start | bytes 786440 | tf_op jit(solution)/shard_map/ppermute | solution.py:16
  110.1 14.5 %collective-permute-start.1 = (f32[128,512]{1,0:T(8,128)S(1)}, f32[128,512]{1,0:T(8,128)S(1)}, u32[]{:S(2)}, u32[]{:S(2)}) collective-permute-start(f32[128,512]{1,0:T(8,128)S(1)} %get-tuple-element.86), channel_id=1, source_target_pairs={{0,4},{4,8},{8,12},{12,16},{16,20},{20,24},{24,28},{1,5},{5,9},{9,... | collective-permute-start | bytes 786440 | tf_op jit(solution)/shard_map/ppermute | solution.py:16
  126.4 42.3 %all-gather.19.cloned.1.call-start = ((), (), s32[]{:S(2)}) async-start(), calls=%async_computation.3 | async-start | bytes 2621440 | tf_op jit(solution)/shard_map/all_gather | solution.py:241
  126.5 15.7 %collective-permute-start.3 = (f32[128,512]{1,0:T(8,128)S(1)}, f32[128,512]{1,0:T(8,128)S(1)}, u32[]{:S(2)}, u32[]{:S(2)}) collective-permute-start(f32[128,512]{1,0:T(8,128)S(1)} %get-tuple-element.59), channel_id=1, source_target_pairs={{0,4},{4,8},{8,12},{12,16},{16,20},{20,24},{24,28},{1,5},{5,9},{9,... | collective-permute-start | bytes 786440 | tf_op jit(solution)/shard_map/ppermute | solution.py:16
  130.9 11.3 %collective-permute-start.4 = (f32[128,512]{1,0:T(8,128)S(1)}, f32[128,512]{1,0:T(8,128)S(1)}, u32[]{:S(2)}, u32[]{:S(2)}) collective-permute-start(f32[128,512]{1,0:T(8,128)S(1)} %get-tuple-element.60), channel_id=1, source_target_pairs={{4,0},{8,4},{12,8},{16,12},{20,16},{24,20},{28,24},{5,1},{9,5},{13... | collective-permute-start | bytes 786440 | tf_op jit(solution)/shard_map/ppermute | solution.py:16
  144.2 61.4 %all-gather.21.cloned.1.call-start = ((), (), s32[]{:S(2)}) async-start(), calls=%async_computation.4 | async-start | bytes 1310720 | tf_op jit(solution)/shard_map/all_gather | solution.py:237
  174.1 12.8 %copy-start.1 = (f32[128,512]{1,0:T(8,128)S(1)}, f32[128,512]{1,0:T(8,128)}, u32[]{:S(2)}) copy-start(f32[128,512]{1,0:T(8,128)} %subtract_subtract_fusion.1) | copy-start | bytes 786436
  175.4 10.3 %collective-permute-start.6 = (f32[128,512]{1,0:T(8,128)S(1)}, f32[128,512]{1,0:T(8,128)S(1)}, u32[]{:S(2)}, u32[]{:S(2)}) collective-permute-start(f32[128,512]{1,0:T(8,128)S(1)} %get-tuple-element.81), channel_id=1, source_target_pairs={{8,0},{12,4},{16,8},{20,12},{24,16},{28,20},{9,1},{13,5},{17,9},{2... | collective-permute-start | bytes 786440 | tf_op jit(solution)/shard_map/ppermute | solution.py:16
  176.7 10.2 %collective-permute-start.5 = (f32[128,512]{1,0:T(8,128)S(1)}, f32[128,512]{1,0:T(8,128)S(1)}, u32[]{:S(2)}, u32[]{:S(2)}) collective-permute-start(f32[128,512]{1,0:T(8,128)S(1)} %get-tuple-element.82), channel_id=1, source_target_pairs={{0,8},{4,12},{8,16},{12,20},{16,24},{20,28},{1,9},{5,13},{9,17},{1... | collective-permute-start | bytes 786440 | tf_op jit(solution)/shard_map/ppermute | solution.py:16
  187.7 43.0 %all-gather.23.cloned.1.call-start = ((), (), s32[]{:S(2)}) async-start(), calls=%async_computation.5 | async-start | bytes 2621440 | tf_op jit(solution)/shard_map/all_gather | solution.py:241
  187.8 9.2 %collective-permute-start.7 = (f32[128,512]{1,0:T(8,128)S(1)}, f32[128,512]{1,0:T(8,128)S(1)}, u32[]{:S(2)}, u32[]{:S(2)}) collective-permute-start(f32[128,512]{1,0:T(8,128)S(1)} %get-tuple-element.67), channel_id=1, source_target_pairs={{0,8},{4,12},{8,16},{12,20},{16,24},{20,28},{1,9},{5,13},{9,17},{1... | collective-permute-start | bytes 786440 | tf_op jit(solution)/shard_map/ppermute | solution.py:16
  192.2 8.9 %collective-permute-start.8 = (f32[128,512]{1,0:T(8,128)S(1)}, f32[128,512]{1,0:T(8,128)S(1)}, u32[]{:S(2)}, u32[]{:S(2)}) collective-permute-start(f32[128,512]{1,0:T(8,128)S(1)} %get-tuple-element.68), channel_id=1, source_target_pairs={{8,0},{12,4},{16,8},{20,12},{24,16},{28,20},{9,1},{13,5},{17,9},{2... | collective-permute-start | bytes 786440 | tf_op jit(solution)/shard_map/ppermute | solution.py:16
  236.1 29.3 %copy-start = (f32[128,512]{1,0:T(8,128)S(1)}, f32[128,512]{1,0:T(8,128)}, u32[]{:S(2)}) copy-start(f32[128,512]{1,0:T(8,128)} %subtract_subtract_fusion) | copy-start | bytes 786436
  237.3 23.2 %collective-permute-start.11 = (f32[128,512]{1,0:T(8,128)S(1)}, f32[128,512]{1,0:T(8,128)S(1)}, u32[]{:S(2)}, u32[]{:S(2)}) collective-permute-start(f32[128,512]{1,0:T(8,128)S(1)} %get-tuple-element.76), channel_id=1, source_target_pairs={{16,0},{20,4},{24,8},{28,12},{17,1},{21,5},{25,9},{29,13},{18,2},{... | collective-permute-start | bytes 786440 | tf_op jit(solution)/shard_map/ppermute | solution.py:16
  238.6 26.8 %collective-permute-start.10 = (f32[128,512]{1,0:T(8,128)S(1)}, f32[128,512]{1,0:T(8,128)S(1)}, u32[]{:S(2)}, u32[]{:S(2)}) collective-permute-start(f32[128,512]{1,0:T(8,128)S(1)} %get-tuple-element.77), channel_id=1, source_target_pairs={{16,0},{20,4},{24,8},{28,12},{17,1},{21,5},{25,9},{29,13},{18,2},{... | collective-permute-start | bytes 786440 | tf_op jit(solution)/shard_map/ppermute | solution.py:16
  239.9 25.5 %collective-permute-start.9 = (f32[128,512]{1,0:T(8,128)S(1)}, f32[128,512]{1,0:T(8,128)S(1)}, u32[]{:S(2)}, u32[]{:S(2)}) collective-permute-start(f32[128,512]{1,0:T(8,128)S(1)} %get-tuple-element.78), channel_id=1, source_target_pairs={{0,16},{4,20},{8,24},{12,28},{1,17},{5,21},{9,25},{13,29},{2,18},{... | collective-permute-start | bytes 786440 | tf_op jit(solution)/shard_map/ppermute | solution.py:16
Sparse Core Ops, SparseCore 0:
  25.4 22.7 all-gather.14
  50.4 21.8 all-gather.12
  126.5 16.7 all-gather.16
  144.8 22.6 all-gather.18
  187.8 17.7 all-gather.20
  207.0 22.5 all-gather.22

commit v3 on v2

--- a/solution.py
+++ b/solution.py
@@ -84,7 +84,7 @@
     return jnp.where(down >= across, out, 0.0)
 
 
-def factor_kernel(diag_ref, high, low, work):
+def factor_kernel(diag_ref, high, low, work, beside=None):
     blocks, rows, order = diag_ref.shape
     work[...] = diag_ref[...]
     for i in range(blocks):
@@ -99,6 +99,8 @@
 
     def step(j, carry):
         at = pl.ds(pl.multiple_of(j * rows, rows), rows)
+        if beside is not None:
+            beside(j)
         inverse = factor_inverse(work[j, :, at])
         work[j, :, at] = unit
         solved = dot3(split(inverse), split(work[j]), 1)
@@ -136,6 +138,10 @@
 
 
 def term_kernel(index_ref, inverse_high, inverse_low, parts_ref, out_ref, high, low):
+    put_terms(index_ref[0], inverse_high, inverse_low, parts_ref, out_ref, high, low)
+
+
+def put_terms(index, inverse_high, inverse_low, parts_ref, out_ref, high, low):
     blocks, _, rows, order = parts_ref.shape
     for part in range(2):
         across = slice(part * order, (part + 1) * order)
@@ -148,7 +154,7 @@
             solved_high, solved_low = split(solved)
             high[at, across] = solved_high
             low[at, across] = solved_low
-    mine = index_ref[0] * rows
+    mine = index * rows
     for k, (first, second) in enumerate(((0, 0), (0, 1), (1, 1), (1, 0))):
         cut = pl.ds(pl.multiple_of(first * order + mine, rows), rows)
         across = slice(second * order, (second + 1) * order)
@@ -166,6 +172,228 @@
         scratch_shapes=[pltpu.VMEM((order, 2 * order), jnp.bfloat16)] * 2,
         cost_estimate=pl.CostEstimate(flops=4000000000, bytes_accessed=16 * order * order, transcendentals=0),
     )(index, *inverse, parts)
+
+
+MESH = pl.DeviceIdType.MESH
+
+
+def across(place, bit):
+    return place + bit - 2 * bit * ((place // bit) % 2)
+
+
+class Spread:
+    def __init__(self, size, place, block, send_sem, recv_sem):
+        bits = [size >> (k + 1) for k in range(size.bit_length() - 1)]
+        self.plan = [(b, 0) for b in bits]
+        for k, b in enumerate(bits):
+            earlier = [0]
+            for e in bits[:k]:
+                earlier += [m + e for m in earlier]
+            self.plan += [(b, m) for m in earlier if m]
+        self.copies, self.arrived = [], set()
+        for k, (b, m) in enumerate(self.plan):
+            held = place
+            for e in bits:
+                if m & e:
+                    held = across(held, e)
+            self.copies.append(
+                pltpu.make_async_remote_copy(
+                    src_ref=block.at[held],
+                    dst_ref=block.at[held],
+                    send_sem=send_sem.at[k],
+                    recv_sem=recv_sem.at[k],
+                    device_id={"swath": across(place, b)},
+                    device_id_type=MESH,
+                )
+            )
+
+    def start_own(self):
+        for copy, (b, m) in zip(self.copies, self.plan):
+            if m == 0:
+                copy.start()
+
+    def forward(self):
+        for copy, (b, m) in zip(self.copies, self.plan):
+            if m:
+                last = m & -m
+                source = self.plan.index((last, m - last))
+                if source not in self.arrived:
+                    self.copies[source].wait_recv()
+                    self.arrived.add(source)
+                copy.start()
+
+    def finish(self):
+        for k, copy in enumerate(self.copies):
+            if k not in self.arrived:
+                copy.wait_recv()
+        for copy in self.copies:
+            copy.wait_send()
+
+
+def greet(distance, times, size, spread_too):
+    place, me = lax.axis_index("swath"), lax.axis_index("tm")
+    barrier = pltpu.get_barrier_semaphore()
+    behind, ahead = me >= distance, me + distance < times
+
+    @pl.when(behind)
+    def _():
+        pl.semaphore_signal(barrier, inc=1, device_id={"tm": me - distance}, device_id_type=MESH)
+
+    @pl.when(ahead)
+    def _():
+        pl.semaphore_signal(barrier, inc=1, device_id={"tm": me + distance}, device_id_type=MESH)
+
+    count = behind.astype(jnp.int32) + ahead.astype(jnp.int32)
+    if spread_too:
+        bits = [size >> (k + 1) for k in range(size.bit_length() - 1)]
+        for b in bits:
+            pl.semaphore_signal(
+                barrier, inc=1, device_id={"swath": across(place, b)}, device_id_type=MESH
+            )
+        count = count + len(bits)
+    pl.semaphore_wait(barrier, count)
+    return place, me, behind, ahead
+
+
+def handed(me, distance, behind, ahead, moves, send_sem, recv_sem):
+    plan = []
+    for k, (source, target, up) in enumerate(moves):
+        copy = pltpu.make_async_remote_copy(
+            src_ref=source,
+            dst_ref=target,
+            send_sem=send_sem.at[k],
+            recv_sem=recv_sem.at[k],
+            device_id={"tm": me + distance if up else me - distance},
+            device_id_type=MESH,
+        )
+        plan.append((copy, target, ahead if up else behind, behind if up else ahead))
+
+    def start(items):
+        for copy, target, sends, receives in items:
+            pl.when(sends)(copy.start)
+
+    def receive(items):
+        for copy, target, sends, receives in items:
+            pl.when(receives)(copy.wait_recv)
+
+            @pl.when(jnp.logical_not(receives))
+            def _():
+                target[...] = jnp.zeros(target.shape, target.dtype)
+
+    def sent(items):
+        for copy, target, sends, receives in items:
+            pl.when(sends)(copy.wait_send)
+
+    return plan, start, receive, sent
+
+
+def step_kernel(distance, times, size, terms_ref, diag_ref, out_ref, out_diag_ref, land, diag_full,
+                parts, high, low, work, solved_high, solved_low, move_send, move_recv,
+                diag_send, diag_recv, part_send, part_recv):
+    place, me, behind, ahead = greet(distance, times, size, True)
+    moves = [
+        (terms_ref.at[0], land.at[0], True),
+        (terms_ref.at[2], land.at[1], False),
+        (terms_ref.at[3], parts.at[place, 0], False),
+        (terms_ref.at[1], parts.at[place, 1], True),
+    ]
+    plan, start, receive, sent = handed(
+        me, distance, behind, ahead, moves, move_send, move_recv
+    )
+    start(plan)
+    receive(plan[:2])
+    mine = diag_ref[...] - land[0] - land[1]
+    out_diag_ref[...] = mine
+    diag_full[place] = mine
+    spread = Spread(size, place, diag_full, diag_send, diag_recv)
+    spread.start_own()
+    spread.forward()
+    spread.finish()
+    part_spread = Spread(size, place, parts, part_send, part_recv)
+    blocks = diag_full.shape[0]
+
+    def beside(j):
+        @pl.when(j == 1)
+        def _():
+            receive(plan[2:])
+            part_spread.start_own()
+
+        @pl.when(j == blocks - 1)
+        def _():
+            part_spread.forward()
+
+    factor_kernel(diag_full, high, low, work, beside)
+    part_spread.finish()
+    sent(plan)
+    put_terms(place, high, low, parts, out_ref, solved_high, solved_low)
+
+
+def step(distance, terms_in, diag_rows):
+    times, size = lax.axis_size("tm"), lax.axis_size("swath")
+    rows, order = diag_rows.shape
+    vmem = pl.BlockSpec(memory_space=pltpu.VMEM)
+    dma = pltpu.SemaphoreType.DMA
+    return pl.pallas_call(
+        functools.partial(step_kernel, distance, times, size),
+        out_shape=(
+            jax.ShapeDtypeStruct((4, rows, order), jnp.float32),
+            jax.ShapeDtypeStruct((rows, order), jnp.float32),
+        ),
+        in_specs=[vmem] * 2,
+        out_specs=(vmem,) * 2,
+        scratch_shapes=[
+            pltpu.VMEM((2, rows, order), jnp.float32),
+            pltpu.VMEM((size, rows, order), jnp.float32),
+            pltpu.VMEM((size, 2, rows, order), jnp.float32),
+            pltpu.VMEM((order, order), jnp.bfloat16),
+            pltpu.VMEM((order, order), jnp.bfloat16),
+            pltpu.VMEM((size, rows, order), jnp.float32),
+            pltpu.VMEM((order, 2 * order), jnp.bfloat16),
+            pltpu.VMEM((order, 2 * order), jnp.bfloat16),
+            dma((4,)),
+            dma((4,)),
+            dma((size - 1,)),
+            dma((size - 1,)),
+            dma((size - 1,)),
+            dma((size - 1,)),
+        ],
+        compiler_params=pltpu.CompilerParams(collective_id=distance, has_side_effects=True),
+    )(terms_in, diag_rows)
+
+
+def last_kernel(distance, times, size, terms_ref, diag_ref, out_diag_ref, out_coup_ref, land, move_send, move_recv):
+    place, me, behind, ahead = greet(distance, times, size, False)
+    moves = [
+        (terms_ref.at[3], land.at[2], False),
+        (terms_ref.at[0], land.at[0], True),
+        (terms_ref.at[2], land.at[1], False),
+    ]
+    plan, start, receive, sent = handed(
+        me, distance, behind, ahead, moves, move_send, move_recv
+    )
+    start(plan)
+    receive(plan)
+    out_coup_ref[...] = -land[2]
+    out_diag_ref[...] = diag_ref[...] - land[0] - land[1]
+    sent(plan)
+
+
+def last(distance, terms_in, diag_rows):
+    times, size = lax.axis_size("tm"), lax.axis_size("swath")
+    rows, order = diag_rows.shape
+    vmem = pl.BlockSpec(memory_space=pltpu.VMEM)
+    return pl.pallas_call(
+        functools.partial(last_kernel, distance, times, size),
+        out_shape=(jax.ShapeDtypeStruct((rows, order), jnp.float32),) * 2,
+        in_specs=[vmem] * 2,
+        out_specs=(vmem,) * 2,
+        scratch_shapes=[
+            pltpu.VMEM((3, rows, order), jnp.float32),
+            pltpu.SemaphoreType.DMA((3,)),
+            pltpu.SemaphoreType.DMA((3,)),
+        ],
+        compiler_params=pltpu.CompilerParams(collective_id=distance, has_side_effects=True),
+    )(terms_in, diag_rows)
 
 
 def slots(scaled, wanted, named, slot_count):
@@ -226,22 +454,11 @@
         [m.reshape(swath_size, row_count, order) for m in (current, previous.T)], axis=1
     )
     index = swath_index.reshape(1).astype(jnp.int32)
-    for level in range(LEVELS):
-        distance = 2**level
-        out = terms(index, factor(full_diag), parts)
-        left_term = passed_along(out[0], "tm", distance)
-        right_term = passed_along(out[2], "tm", -distance)
-        diag_rows = diag_rows - left_term - right_term
-        if level < LEVELS - 1:
-            diag_rows, across, back = lax.optimization_barrier((diag_rows, out[1], out[3]))
-            full_diag = lax.all_gather(diag_rows, "swath", axis=0)
-            ahead = passed_along(across, "tm", distance)
-            coup_rows = passed_along(back, "tm", -distance)
-            full_diag, ahead, coup_rows = lax.optimization_barrier((full_diag, ahead, coup_rows))
-            parts = lax.all_gather(jnp.stack([coup_rows, ahead]), "swath", axis=0)
-        else:
-            coup_rows = passed_along(out[3], "tm", -distance)
-    return (diag_rows[None], -coup_rows[None])
+    out = terms(index, factor(full_diag), parts)
+    for level in range(LEVELS - 1):
+        out, diag_rows = step(2**level, out, diag_rows)
+    diag_rows, coup_rows = last(2 ** (LEVELS - 1), out, diag_rows)
+    return (diag_rows[None], coup_rows[None])
 
 
 def solution(mesh):

time: 274 us -> 254 us (0.927)
  Pallas kernels: 89 us -> 163 us
  waiting for transfers between devices: 83.1 us -> 25 us
  starting transfers between devices: 36.7 us -> 5 us
  other arithmetic: 15.3 us -> 9.66 us
    pallas_call x0 -> x3, Pallas kernels: none -> 133 us  [the longest x2 105 us: step(): pl.pallas_call(functools.partial(step_kernel, distance, times, size), out...]
    ppermute x12 -> x1, waiting for transfers between devices: 60.6 us -> 8.33 us  [passed_along(): return lax.ppermute(block, axis, route)]
    pallas_call x3 -> x1, Pallas kernels: 72.7 us -> 24.2 us  [factor(): pl.pallas_call(factor_kernel, out_shape=(out, out), in_specs=[pl.BlockSpe...]
    ppermute x12 -> x1, starting transfers between devices: 36.3 us -> 4.92 us  [passed_along(): return lax.ppermute(block, axis, route)]
    pallas_call x3 -> x1, Pallas kernels: 16.3 us -> 5.4 us  [terms(): pl.pallas_call(term_kernel, out_shape=jax.ShapeDtypeStruct((4, rows, orde...]
    all_gather x4 -> x0, waiting for transfers between devices: 5.68 us -> none  [the longest x2 5.68 us: shards(): full_diag = lax.all_gather(diag_rows, 'swath', axis=0)]
    squeeze x3 -> x0, local copies, waits for them, and re-layouts: 3.76 us -> none  [the longest x2 2.55 us: shards(): out[3]]
    unnamed x12 -> x10, local copies, waits for them, and re-layouts: 1.22 us -> 4.56 us
  transfers between devices with their start and end apart: 18 -> 3, of which waited for: 13 -> 2; matrix products, arithmetic and copies ran while one was open for 3% -> 2% of each run, Pallas kernels for 18% -> 0%
where the time goes in v3:
time: 254 us; the launch traced here: 253 us
  Pallas kernels  163 us (64%)
  between operations  35.4 us (14%)
  waiting for transfers between devices  25 us (10%)
  local copies, waits for them, and re-layouts  10.1 us (4%)
  other arithmetic  9.66 us (4%)
  matrix products  5.11 us (2%)
  starting transfers between devices  5 us (2%)
    pallas_call x2, Pallas kernels, step(): pl.pallas_call(functools.partial(step_kernel, distance, times, size), out...  105 us
    pallas_call x1, Pallas kernels, last(): pl.pallas_call(functools.partial(last_kernel, distance, times, size), out...  28 us
    pallas_call x1, Pallas kernels, factor(): pl.pallas_call(factor_kernel, out_shape=(out, out), in_specs=[pl.BlockSpe...  24.2 us
    all_gather x1, waiting for transfers between devices, shards(): far = lax.all_gather(arrived, 'swath', axis=0)  16.6 us
    ppermute x1, waiting for transfers between devices, passed_along(): return lax.ppermute(block, axis, route)  8.33 us
    pallas_call x1, Pallas kernels, terms(): pl.pallas_call(term_kernel, out_shape=jax.ShapeDtypeStruct((4, rows, orde...  5.4 us
    dot_general x2, matrix products, shards(): lax.dot_general(w, w, (((0,), (0,)), ((), ())), preferred_element_type=jn...  5.11 us
  transfers between devices with their start and end apart: 3, of which 2 were waited for; matrix products, arithmetic and copies ran while one was open for 2% of the time, Pallas kernels for 0%

profile of v3, /device:TPU:0, one launch (start us, length us, event | category | flops | bytes accessed | tf_op | source)
XLA Modules:
  0.0 252.9 jit_solution(14158308076010154966)
XLA Ops:
  7.2 0.7 fusion.12
  7.9 0.2 reduce-window.19
  8.1 0.7 fusion.16
  14.1 0.7 subtract_reduce-precision_fusion
  14.8 1.2 multiply_reduce_fusion
  16.7 0.7 bitcast_and_fusion.1
  17.3 0.7 fusion.15
  23.1 0.2 scatter.11
  23.3 1.2 broadcast_multiply_fusion
  24.9 0.8 pad_maximum_fusion.1
  25.7 0.2 reduce-window.18
  25.9 0.7 fusion.14
  36.8 4.9 %collective-permute-start = (bf16[384,512]{1,0:T(8,128)(2,1)S(1)}, bf16[384,512]{1,0:T(8,128)(2,1)S(1)}, u32[]{:S(2)}, u32[]{:S(2)}) collective-permute-start(bf16[384,512]{1,0:T(8,128)(2,1)S(1)} %pad_maximum_fusion.2), channel_id=1, source_target_pairs={{0,4},{4,8},{8,12},{12,16},{16,20},{20,24},{24,28},{1,5},{5,9},{9,... | collective-permute-start | bytes 1179656 | tf_op jit(solution)/shard_map/ppermute | solution.py:16
  41.8 8.3 %collective-permute-done = bf16[384,512]{1,0:T(8,128)(2,1)S(1)} collective-permute-done((bf16[384,512]{1,0:T(8,128)(2,1)S(1)}, bf16[384,512]{1,0:T(8,128)(2,1)S(1)}, u32[]{:S(2)}, u32[]{:S(2)}) %collective-permute-start) | collective-permute-done | bytes 393248 | tf_op jit(solution)/shard_map/ppermute | solution.py:16
  50.1 0.8 copy-done.1
  50.9 0.7 slice_convert_fusion.1
  51.6 3.3 %convolution_bitcast_fusion.1 = f32[512,512]{1,0:T(8,128)} fusion(bf16[4,400,512]{2,1,0:T(8,128)(2,1)} %bitcast.90), kind=kOutput, calls=%fused_computation.2 | convolution fusion | flops 536870912 | bytes 2097152 | tf_op jit(solution)/shard_map/dot_general | solution.py:442
  55.0 1.3 fusion.7
  56.2 16.6 %all-gather.5.cloned.1.call-done = bf16[1536,512]{1,0:T(8,128)(2,1)} async-done(((bf16[384,512]{1,0:T(8,128)(2,1)}), bf16[1536,512]{1,0:T(8,128)(2,1)}) %all-gather.5.cloned.1.call-update) | async-done | bytes 1572880 | tf_op jit(solution)/shard_map/all_gather | solution.py:440
  72.9 1.2 slice.206
  74.4 0.3 copy-done.3
  74.7 1.8 fusion.2
  76.5 24.2 %shard_map.68 = (bf16[512,512]{1,0:T(8,128)(2,1)}, bf16[512,512]{1,0:T(8,128)(2,1)}) custom-call(f32[4,128,512]{2,1,0:T(8,128)} %bitcast.92), custom_call_target="tpu_custom_call" | custom-call | flops 20000000000 | bytes 1048576 | tf_op jit(solution)/shard_map/pallas_call | solution.py:130
  100.7 0.3 copy.12
  101.1 1.7 constant_dynamic-slice_fusion.diag_ref
  102.7 1.6 pad_maximum_fusion.parts_ref
  104.4 5.4 %shard_map.69.terms_ref = f32[4,128,512]{2,1,0:T(8,128)} custom-call(s32[1]{0:T(128)} %bitcast.index_ref, bf16[512,512]{1,0:T(8,128)(2,1)} %get-tuple-element.46.inverse_high, bf16[512,512]{1,0:T(8,128)(2,1)} %get-tuple-element.47.inverse_low, f32[4,2,128,512]{3,2,1,0:T(8,128)} %pad_maximum_fusion.parts_ref), custom_call_target="tpu_custom_call" | custom-call | flops 4000000000 | bytes 4194304 | tf_op jit(solution)/shard_map/pallas_call | solution.py:166
  109.8 46.9 %shard_map.70 = (f32[4,128,512]{2,1,0:T(8,128)}, f32[128,512]{1,0:T(8,128)}) custom-call(f32[4,128,512]{2,1,0:T(8,128)} %shard_map.69.terms_ref, f32[128,512]{1,0:T(8,128)} %constant_dynamic-slice_fusion.diag_ref), custom_call_target="tpu_custom_call" | custom-call | tf_op jit(solution)/shard_map/pallas_call | solution.py:336
  156.7 58.1 %shard_map.71 = (f32[4,128,512]{2,1,0:T(8,128)}, f32[128,512]{1,0:T(8,128)}) custom-call(f32[4,128,512]{2,1,0:T(8,128)} %get-tuple-element.48.terms_ref, f32[128,512]{1,0:T(8,128)} %get-tuple-element.49.diag_ref), custom_call_target="tpu_custom_call" | custom-call | tf_op jit(solution)/shard_map/pallas_call | solution.py:336
  214.7 28.0 %shard_map.72 = (f32[128,512]{1,0:T(8,128)}, f32[128,512]{1,0:T(8,128)}) custom-call(f32[4,128,512]{2,1,0:T(8,128)} %get-tuple-element.50.terms_ref, f32[128,512]{1,0:T(8,128)} %get-tuple-element.51.diag_ref), custom_call_target="tpu_custom_call" | custom-call | tf_op jit(solution)/shard_map/pallas_call | solution.py:385
  242.7 1.7 copy.18
  244.4 1.7 copy.19
  (21 shorter events, 0.9 us)
Async XLA Ops:
  7.2 17.7 %copy-start = (bf16[1,128,512]{2,1,0:T(8,128)(2,1)S(1)}, bf16[1,128,512]{2,1,0:T(8,128)(2,1)}, u32[]{:S(2)}) copy-start(bf16[1,128,512]{2,1,0:T(8,128)(2,1)} %param.12) | copy-start | bytes 393220
  7.2 43.7 %all-gather.7.cloned.1.call-start = ((), (), s32[]{:S(2)}) async-start(), calls=%async_computation.1 | async-start | bytes 2048000 | tf_op jit(solution)/shard_map/all_gather | solution.py:439
  25.7 47.2 %all-gather.5.cloned.1.call-start = ((), (), s32[]{:S(2)}) async-start(), calls=%async_computation | async-start | bytes 1966080 | tf_op jit(solution)/shard_map/all_gather | solution.py:440
  36.8 13.3 %collective-permute-start = (bf16[384,512]{1,0:T(8,128)(2,1)S(1)}, bf16[384,512]{1,0:T(8,128)(2,1)S(1)}, u32[]{:S(2)}, u32[]{:S(2)}) collective-permute-start(bf16[384,512]{1,0:T(8,128)(2,1)S(1)} %pad_maximum_fusion.2), channel_id=1, source_target_pairs={{0,4},{4,8},{8,12},{12,16},{16,20},{20,24},{24,28},{1,5},{5,9},{9,... | collective-permute-start | bytes 1179656 | tf_op jit(solution)/shard_map/ppermute | solution.py:16
  50.1 0.8 copy-start.1
  72.9 1.6 copy-start.2
  72.9 1.9 copy-start.3
Sparse Core Ops, SparseCore 0:
  25.8 22.7 all-gather.6
  51.0 21.8 all-gather.4

commit v4 on v3

--- a/solution.py
+++ b/solution.py
@@ -8,12 +8,6 @@
 from jax.sharding import PartitionSpec as P
 
 LEVELS = 3
-
-
-def passed_along(block, axis, distance):
-    devices = range(lax.axis_size(axis))
-    route = [(i - distance, i) for i in devices if i - distance in devices]
-    return lax.ppermute(block, axis, route)
 
 
 def split(x):
@@ -124,23 +118,6 @@
     lax.fori_loop(0, blocks, step, 0)
 
 
-def factor(diag):
-    blocks, rows, order = diag.shape
-    out = jax.ShapeDtypeStruct((order, order), jnp.bfloat16)
-    return pl.pallas_call(
-        factor_kernel,
-        out_shape=(out, out),
-        in_specs=[pl.BlockSpec(memory_space=pltpu.VMEM)],
-        out_specs=(pl.BlockSpec(memory_space=pltpu.VMEM),) * 2,
-        scratch_shapes=[pltpu.VMEM((blocks, rows, order), jnp.float32)],
-        cost_estimate=pl.CostEstimate(flops=20000000000, bytes_accessed=4 * order * order, transcendentals=0),
-    )(diag)
-
-
-def term_kernel(index_ref, inverse_high, inverse_low, parts_ref, out_ref, high, low):
-    put_terms(index_ref[0], inverse_high, inverse_low, parts_ref, out_ref, high, low)
-
-
 def put_terms(index, inverse_high, inverse_low, parts_ref, out_ref, high, low):
     blocks, _, rows, order = parts_ref.shape
     for part in range(2):
@@ -161,19 +138,6 @@
         out_ref[k] = dot3((high[:, cut], low[:, cut]), (high[:, across], low[:, across]), 0)
 
 
-def terms(index, inverse, parts):
-    blocks, _, rows, order = parts.shape
-    return pl.pallas_call(
-        term_kernel,
-        out_shape=jax.ShapeDtypeStruct((4, rows, order), jnp.float32),
-        in_specs=[pl.BlockSpec(memory_space=pltpu.SMEM)]
-        + [pl.BlockSpec(memory_space=pltpu.VMEM)] * 3,
-        out_specs=pl.BlockSpec(memory_space=pltpu.VMEM),
-        scratch_shapes=[pltpu.VMEM((order, 2 * order), jnp.bfloat16)] * 2,
-        cost_estimate=pl.CostEstimate(flops=4000000000, bytes_accessed=16 * order * order, transcendentals=0),
-    )(index, *inverse, parts)
-
-
 MESH = pl.DeviceIdType.MESH
 
 
@@ -182,7 +146,7 @@
 
 
 class Spread:
-    def __init__(self, size, place, block, send_sem, recv_sem):
+    def __init__(self, size, place, block, send_sem, recv_sem, own=None):
         bits = [size >> (k + 1) for k in range(size.bit_length() - 1)]
         self.plan = [(b, 0) for b in bits]
         for k, b in enumerate(bits):
@@ -198,7 +162,7 @@
                     held = across(held, e)
             self.copies.append(
                 pltpu.make_async_remote_copy(
-                    src_ref=block.at[held],
+                    src_ref=own if own is not None and m == 0 else block.at[held],
                     dst_ref=block.at[held],
                     send_sem=send_sem.at[k],
                     recv_sem=recv_sem.at[k],
@@ -300,8 +264,9 @@
     plan, start, receive, sent = handed(
         me, distance, behind, ahead, moves, move_send, move_recv
     )
-    start(plan)
+    start(plan[:2])
     receive(plan[:2])
+    start(plan[2:])
     mine = diag_ref[...] - land[0] - land[1]
     out_diag_ref[...] = mine
     diag_full[place] = mine
@@ -396,67 +361,145 @@
     )(terms_in, diag_rows)
 
 
-def slots(scaled, wanted, named, slot_count):
-    place = jnp.cumsum(named.astype(jnp.int32)) - 1
-    out = []
-    for slot in range(slot_count):
-        chosen = jnp.zeros(scaled.shape[1:], jnp.float32)
-        for r in range(scaled.shape[0]):
-            chosen = jnp.where(wanted[r] & (place[r] == slot), scaled[r], chosen)
-        out.append(chosen)
-    return jnp.concatenate(out, axis=0).astype(jnp.bfloat16)
+def weigh_kernel(total_slots, block_rows, design_ref, process_ref, routes_ref, counts_ref, near_ref, sent_ref):
+    me = lax.axis_index("tm")
+    block_count = routes_ref.shape[1]
+    slot_count = block_count // 2
+    weighted = []
+    for r in range(block_count):
+        raw = design_ref[r * block_rows : (r + 1) * block_rows, :].astype(jnp.float32)
+        mean_sq = jnp.mean(raw * raw, axis=-1, keepdims=True)
+        weighted.append((raw * lax.rsqrt(4.0 * total_slots * (mean_sq + 1e-06))).astype(jnp.bfloat16))
+    for out_ref, owner in ((near_ref, me), (sent_ref, me + 1)):
+        place = jnp.int32(0)
+        chosen = [jnp.full((), -1, jnp.int32) for _ in range(slot_count)]
+        for r in range(block_count):
+            named = routes_ref[0, r] == owner
+            live = r < counts_ref[0, 0]
+            for k in range(slot_count):
+                chosen[k] = jnp.where(named & live & (place == k), r, chosen[k])
+            place = place + named.astype(jnp.int32)
+        for k in range(slot_count):
+            block = jnp.zeros(weighted[0].shape, jnp.float32)
+            for r in range(block_count):
+                block = jnp.where(chosen[k] == r, weighted[r].astype(jnp.float32), block)
+            out_ref[k * block_rows : (k + 1) * block_rows, :] = block.astype(jnp.bfloat16)
+        out_ref[slot_count * block_rows :, :] = process_ref[...]
+
+
+def weigh(design, process, routes, counts, total_slots):
+    order = process.shape[1]
+    block_count = routes.shape[1]
+    block_rows = design.shape[0] // block_count
+    rows = block_count // 2 * block_rows + process.shape[0]
+    vmem, smem = (pl.BlockSpec(memory_space=m) for m in (pltpu.VMEM, pltpu.SMEM))
+    return pl.pallas_call(
+        functools.partial(weigh_kernel, total_slots, block_rows),
+        out_shape=(jax.ShapeDtypeStruct((rows, order), jnp.bfloat16),) * 2,
+        in_specs=[vmem, vmem, smem, smem],
+        out_specs=(vmem,) * 2,
+    )(design, process, routes, counts)
+
+
+def first_kernel(times, size, near_ref, sent_ref, prior_ref, out_ref, out_diag_ref, near, far, prior,
+                 diag_full, parts, high, low, work, solved_high, solved_low, move_send, move_recv,
+                 near_send, near_recv, prior_send, prior_recv, far_send, far_recv):
+    place, me, behind, ahead = greet(1, times, size, True)
+    rows, order = diag_full.shape[1:]
+    observed = near.shape[1] - rows
+    plan, start, receive, sent = handed(
+        me, 1, behind, ahead, [(sent_ref, far.at[place], True)], move_send, move_recv
+    )
+    start(plan)
+    near_spread = Spread(size, place, near, near_send, near_recv, near_ref)
+    prior_spread = Spread(size, place, prior, prior_send, prior_recv, prior_ref)
+    near_spread.start_own()
+    prior_spread.start_own()
+    near[place] = near_ref[...]
+    prior[place] = prior_ref[...]
+    receive(plan)
+    far_spread = Spread(size, place, far, far_send, far_recv)
+    far_spread.start_own()
+    near_spread.forward()
+    prior_spread.forward()
+    near_spread.finish()
+    prior_spread.finish()
+    far_spread.forward()
+    square = (rows, rows)
+    unit = lax.broadcasted_iota(jnp.int32, square, 0) == lax.broadcasted_iota(jnp.int32, square, 1)
+
+    def add_grams(source):
+        for b in range(size):
+            cut = slice(b * rows, (b + 1) * rows)
+            total = source[b, observed:].astype(jnp.float32)
+            for i in range(size):
+                total = total + lax.dot_general(
+                    source[i, :observed, cut],
+                    source[i, :observed, :],
+                    (((0,), (0,)), ((), ())),
+                    preferred_element_type=jnp.float32,
+                )
+            yield b, cut, total
+
+    for b, cut, total in add_grams(near):
+        diag_full[b] = total
+        diag_full[b, :, cut] += jnp.where(unit, jnp.broadcast_to(prior[b][:1], square), 0.0)
+        parts[b, 0] = near[b, observed:].astype(jnp.float32)
+    far_spread.finish()
+    for b, cut, total in add_grams(far):
+        diag_full[b] += total
+        for q in range(size):
+            turned = far[q, observed:, cut].astype(jnp.float32).T
+            parts[b, 1, :, q * rows : (q + 1) * rows] = turned
+    out_diag_ref[...] = diag_full[place]
+    factor_kernel(diag_full, high, low, work)
+    sent(plan)
+    put_terms(place, high, low, parts, out_ref, solved_high, solved_low)
+
+
+def first(near, sent, prior):
+    times, size = lax.axis_size("tm"), lax.axis_size("swath")
+    order = near.shape[1]
+    rows = order // size
+    vmem = pl.BlockSpec(memory_space=pltpu.VMEM)
+    dma = pltpu.SemaphoreType.DMA
+    return pl.pallas_call(
+        functools.partial(first_kernel, times, size),
+        out_shape=(
+            jax.ShapeDtypeStruct((4, rows, order), jnp.float32),
+            jax.ShapeDtypeStruct((rows, order), jnp.float32),
+        ),
+        in_specs=[vmem] * 3,
+        out_specs=(vmem,) * 2,
+        scratch_shapes=[
+            pltpu.VMEM((size,) + near.shape, jnp.bfloat16),
+            pltpu.VMEM((size,) + near.shape, jnp.bfloat16),
+            pltpu.VMEM((size,) + prior.shape, jnp.float32),
+            pltpu.VMEM((size, rows, order), jnp.float32),
+            pltpu.VMEM((size, 2, rows, order), jnp.float32),
+            pltpu.VMEM((order, order), jnp.bfloat16),
+            pltpu.VMEM((order, order), jnp.bfloat16),
+            pltpu.VMEM((size, rows, order), jnp.float32),
+            pltpu.VMEM((order, 2 * order), jnp.bfloat16),
+            pltpu.VMEM((order, 2 * order), jnp.bfloat16),
+            dma((1,)),
+            dma((1,)),
+        ]
+        + [dma((size - 1,))] * 6,
+        compiler_params=pltpu.CompilerParams(collective_id=0, has_side_effects=True),
+    )(near, sent, prior)
 
 
 def shards(design, process, prior_prec, routes, counts):
     row_count = process.shape[1]
-    order = process.shape[2]
-    my_time = lax.axis_index("tm")
-    swath_index = lax.axis_index("swath")
-    swath_size = lax.axis_size("swath")
     block_count = routes.shape[1]
-    slot_count = block_count // 2
     block_rows = design.shape[1] // block_count
-    total_slots = 2 * slot_count * block_rows * swath_size
-    row_start = swath_index * row_count
-    raw_rows = design[0].reshape(block_count, block_rows, order).astype(jnp.float32)
-    mean_sq = jnp.mean(raw_rows * raw_rows, axis=-1, keepdims=True)
-    scaled = raw_rows * lax.rsqrt(4.0 * total_slots * (mean_sq + 1e-06))
-    live = jnp.arange(block_count) < counts[0, 0]
-    target = routes[0]
-    own, ahead = target == my_time, target == my_time + 1
-    own_blocks = slots(scaled, live & own, own, slot_count)
-    ahead_blocks = slots(scaled, live & ahead, ahead, slot_count)
-    sent = jnp.concatenate([ahead_blocks, process[0]], axis=0)
-    arrived = passed_along(sent, "tm", 1)
-    prior = prior_prec[0]
-    first = lax.reduce_precision(prior, 8, 7)
-    second = lax.reduce_precision(prior - first, 8, 7)
-    third = lax.reduce_precision(prior - first - second, 8, 7)
-    pieces = jnp.zeros((16, order), jnp.float32)
-    for i, piece in enumerate((first, second, third)):
-        pieces = pieces.at[i, :row_count].set(piece)
-    near = jnp.concatenate([own_blocks, process[0], pieces.astype(jnp.bfloat16)], axis=0)
-    near = lax.all_gather(near, "swath", axis=0)
-    far = lax.all_gather(arrived, "swath", axis=0)
-    cut = slot_count * block_rows
-    over_rows = lambda w: lax.dot_general(
-        w, w, (((0,), (0,)), ((), ())), preferred_element_type=jnp.float32
-    )
-    previous = far[:, cut:].reshape(order, order).astype(jnp.float32)
-    current = near[:, cut : cut + row_count].reshape(order, order).astype(jnp.float32)
-    three = near[:, cut + row_count : cut + row_count + 3, :row_count].astype(jnp.float32)
-    prior_full = (three[:, 0] + three[:, 1] + three[:, 2]).reshape(order)
-    gram = over_rows(near[:, :cut].reshape(-1, order)) + over_rows(far[:, :cut].reshape(-1, order))
-    full_diag = previous + current + gram + jnp.diag(prior_full)
-    diag_rows = lax.dynamic_slice_in_dim(full_diag, row_start, row_count, 0)
-    full_diag = full_diag.reshape(swath_size, row_count, order)
-    parts = jnp.stack(
-        [m.reshape(swath_size, row_count, order) for m in (current, previous.T)], axis=1
-    )
-    index = swath_index.reshape(1).astype(jnp.int32)
-    out = terms(index, factor(full_diag), parts)
-    for level in range(LEVELS - 1):
-        out, diag_rows = step(2**level, out, diag_rows)
+    total_slots = 2 * (block_count // 2) * block_rows * lax.axis_size("swath")
+    near, sent = weigh(design[0], process[0], routes, counts, total_slots)
+    prior = jnp.broadcast_to(prior_prec, (8, row_count))
+    out, diag_rows = first(near, sent, prior)
+    for level in range(1, LEVELS):
+        out, diag_rows = step(2 ** (level - 1), out, diag_rows)
     diag_rows, coup_rows = last(2 ** (LEVELS - 1), out, diag_rows)
     return (diag_rows[None], coup_rows[None])
 

time: 254 us -> 187 us (0.74)
  between operations: 35.4 us -> 1.33 us
  waiting for transfers between devices: 25 us -> 0 us
  Pallas kernels: 163 us -> 182 us
  other arithmetic: 9.66 us -> 0 us
  local copies, waits for them, and re-layouts: 10.1 us -> 3.66 us
  matrix products: 5.11 us -> 0 us
  starting transfers between devices: 5 us -> 0 us
    pallas_call x2, Pallas kernels: 29.6 us -> 52.9 us  [the longest x1 50.6 us: first(): pl.pallas_call(functools.partial(first_kernel, times, size), out_shape=(j...]
    all_gather x2 -> x0, waiting for transfers between devices: 16.6 us -> none  [the longest x1 16.6 us: shards(): far = lax.all_gather(arrived, 'swath', axis=0)]
    ppermute x1 -> x0, waiting for transfers between devices: 8.33 us -> none  [passed_along(): return lax.ppermute(block, axis, route)]
    dot_general x2 -> x0, matrix products: 5.11 us -> none  [shards(): lax.dot_general(w, w, (((0,), (0,)), ((), ())), preferred_element_type=jn...]
    ppermute x1 -> x0, starting transfers between devices: 4.92 us -> none  [passed_along(): return lax.ppermute(block, axis, route)]
    pallas_call x2, Pallas kernels: 105 us -> 101 us  [step(): pl.pallas_call(functools.partial(step_kernel, distance, times, size), out...]
    slice x4 -> x0, local copies, waits for them, and re-layouts: 3.24 us -> none  [the longest x3 2.01 us: slots(): chosen = jnp.where(wanted[r] & (place[r] == slot), scaled[r], chosen)]
    convert_element_type x3 -> x0, other arithmetic: 2.65 us -> none  [the longest x1 1.29 us: shards(): near[:, cut:cut + row_count].reshape(order, order).astype(jnp.float32)]
  transfers between devices with their start and end apart: 3 -> 0, of which waited for: 2 -> 0; matrix products, arithmetic and copies ran while one was open for 2% -> 0% of each run, Pallas kernels for 0% -> 0%
where the time goes in v4:
time: 187 us
  Pallas kernels  182 us (97%)
  local copies, waits for them, and re-layouts  3.66 us (2%)
    pallas_call x2, Pallas kernels, step(): pl.pallas_call(functools.partial(step_kernel, distance, times, size), out...  101 us
    pallas_call x1, Pallas kernels, first(): pl.pallas_call(functools.partial(first_kernel, times, size), out_shape=(j...  50.6 us
    pallas_call x1, Pallas kernels, last(): pl.pallas_call(functools.partial(last_kernel, distance, times, size), out...  27.9 us

profile of v4, /device:TPU:0, one launch (start us, length us, event | category | flops | bytes accessed | tf_op | source)
XLA Modules:
  0.0 186.6 jit_solution(201846334142520056)
XLA Ops:
  1.3 0.0 copy-start.1
  1.3 0.6 copy-done.1
  1.9 0.6 broadcast_in_dim.14.prior_ref
  2.5 2.3 %shard_map.68 = (bf16[384,512]{1,0:T(8,128)(2,1)}, bf16[384,512]{1,0:T(8,128)(2,1)}) custom-call(bf16[512,512]{1,0:T(8,128)(2,1)} %bitcast.5, bf16[128,512]{1,0:T(8,128)(2,1)} %bitcast.8, s32[1,4]{1,0:T(1,128)} %routes_ref.1, s32[1,1]{1,0:T(1,128)S(6)} %copy.9.counts_ref), custom_call_target="tpu_custom_call" | custom-call | tf_op jit(solution)/shard_map/pallas_call | solution.py:396
  4.9 50.6 %shard_map.69 = (f32[4,128,512]{2,1,0:T(8,128)}, f32[128,512]{1,0:T(8,128)}) custom-call(bf16[384,512]{1,0:T(8,128)(2,1)} %get-tuple-element.12.near_ref, bf16[384,512]{1,0:T(8,128)(2,1)} %get-tuple-element.13.sent_ref, f32[8,128]{1,0:T(8,128)} %broadcast_in_dim.14.prior_ref), custom_call_target="tpu_custom_call" | custom-call | tf_op jit(solution)/shard_map/pallas_call | solution.py:466
  55.5 48.5 %shard_map.70 = (f32[4,128,512]{2,1,0:T(8,128)}, f32[128,512]{1,0:T(8,128)}) custom-call(f32[4,128,512]{2,1,0:T(8,128)} %get-tuple-element.14.terms_ref, f32[128,512]{1,0:T(8,128)} %get-tuple-element.15.diag_ref), custom_call_target="tpu_custom_call" | custom-call | tf_op jit(solution)/shard_map/pallas_call | solution.py:301
  104.0 52.3 %shard_map.71 = (f32[4,128,512]{2,1,0:T(8,128)}, f32[128,512]{1,0:T(8,128)}) custom-call(f32[4,128,512]{2,1,0:T(8,128)} %get-tuple-element.16.terms_ref, f32[128,512]{1,0:T(8,128)} %get-tuple-element.17.diag_ref), custom_call_target="tpu_custom_call" | custom-call | tf_op jit(solution)/shard_map/pallas_call | solution.py:301
  156.3 27.9 %shard_map.72 = (f32[128,512]{1,0:T(8,128)}, f32[128,512]{1,0:T(8,128)}) custom-call(f32[4,128,512]{2,1,0:T(8,128)} %get-tuple-element.18.terms_ref, f32[128,512]{1,0:T(8,128)} %get-tuple-element.19.diag_ref), custom_call_target="tpu_custom_call" | custom-call | tf_op jit(solution)/shard_map/pallas_call | solution.py:350
  184.2 0.0 copy-start
  184.2 1.7 copy.10
  185.9 0.0 copy-done
  185.9 0.7 copy.11
Async XLA Ops:
  1.3 0.7 copy-start.1
  184.2 1.7 copy-start

commit v5 on v4

--- a/solution.py
+++ b/solution.py
@@ -8,6 +8,7 @@
 from jax.sharding import PartitionSpec as P
 
 LEVELS = 3
+PIECES = 2
 
 
 def split(x):
@@ -65,7 +66,7 @@
                 back[k] = back[k] - lower[s, k] * back[s]
         for h in range(g + 1, groups):
             left = jnp.where(inside, 0.0, rows[h])
-            for s in range(width):
+            for s in range(width - 1, -1, -1):
                 left = left - columns[h][s] * back[s]
             rows[h] = left
         group = solved[0]
@@ -146,7 +147,7 @@
 
 
 class Spread:
-    def __init__(self, size, place, block, send_sem, recv_sem, own=None):
+    def __init__(self, size, place, block, send_sem, recv_sem, own=None, cut=None, base=0):
         bits = [size >> (k + 1) for k in range(size.bit_length() - 1)]
         self.plan = [(b, 0) for b in bits]
         for k, b in enumerate(bits):
@@ -155,6 +156,7 @@
                 earlier += [m + e for m in earlier]
             self.plan += [(b, m) for m in earlier if m]
         self.copies, self.arrived = [], set()
+        part = lambda held: block.at[held] if cut is None else block.at[held, cut]
         for k, (b, m) in enumerate(self.plan):
             held = place
             for e in bits:
@@ -162,10 +164,10 @@
                     held = across(held, e)
             self.copies.append(
                 pltpu.make_async_remote_copy(
-                    src_ref=own if own is not None and m == 0 else block.at[held],
-                    dst_ref=block.at[held],
-                    send_sem=send_sem.at[k],
-                    recv_sem=recv_sem.at[k],
+                    src_ref=own if own is not None and m == 0 else part(held),
+                    dst_ref=part(held),
+                    send_sem=send_sem.at[base + k],
+                    recv_sem=recv_sem.at[base + k],
                     device_id={"swath": across(place, b)},
                     device_id_type=MESH,
                 )
@@ -255,32 +257,42 @@
                 parts, high, low, work, solved_high, solved_low, move_send, move_recv,
                 diag_send, diag_recv, part_send, part_recv):
     place, me, behind, ahead = greet(distance, times, size, True)
-    moves = [
-        (terms_ref.at[0], land.at[0], True),
-        (terms_ref.at[2], land.at[1], False),
-        (terms_ref.at[3], parts.at[place, 0], False),
-        (terms_ref.at[1], parts.at[place, 1], True),
-    ]
+    piece = diag_ref.shape[0] // PIECES
+    cuts = [pl.ds(c * piece, piece) for c in range(PIECES)]
+    moves = []
+    for cut in cuts:
+        moves.append((terms_ref.at[0, cut], land.at[0, cut], True))
+        moves.append((terms_ref.at[2, cut], land.at[1, cut], False))
+    moves.append((terms_ref.at[3], parts.at[place, 0], False))
+    moves.append((terms_ref.at[1], parts.at[place, 1], True))
     plan, start, receive, sent = handed(
         me, distance, behind, ahead, moves, move_send, move_recv
     )
-    start(plan[:2])
-    receive(plan[:2])
-    start(plan[2:])
-    mine = diag_ref[...] - land[0] - land[1]
-    out_diag_ref[...] = mine
-    diag_full[place] = mine
-    spread = Spread(size, place, diag_full, diag_send, diag_recv)
-    spread.start_own()
-    spread.forward()
-    spread.finish()
+    coupled = 2 * PIECES
+    start(plan[:coupled])
+    spreads = []
+    for c, cut in enumerate(cuts):
+        receive(plan[2 * c : 2 * c + 2])
+        if c == PIECES - 1:
+            start(plan[coupled:])
+        mine = diag_ref[cut] - land[0, cut] - land[1, cut]
+        out_diag_ref[cut] = mine
+        diag_full[place, cut] = mine
+        spreads.append(
+            Spread(size, place, diag_full, diag_send, diag_recv, None, cut, c * (size - 1))
+        )
+        spreads[c].start_own()
+    for spread in spreads:
+        spread.forward()
+    for spread in spreads:
+        spread.finish()
     part_spread = Spread(size, place, parts, part_send, part_recv)
     blocks = diag_full.shape[0]
 
     def beside(j):
         @pl.when(j == 1)
         def _():
-            receive(plan[2:])
+            receive(plan[coupled:])
             part_spread.start_own()
 
         @pl.when(j == blocks - 1)
@@ -315,10 +327,10 @@
             pltpu.VMEM((size, rows, order), jnp.float32),
             pltpu.VMEM((order, 2 * order), jnp.bfloat16),
             pltpu.VMEM((order, 2 * order), jnp.bfloat16),
-            dma((4,)),
-            dma((4,)),
-            dma((size - 1,)),
-            dma((size - 1,)),
+            dma((2 * PIECES + 2,)),
+            dma((2 * PIECES + 2,)),
+            dma((PIECES * (size - 1),)),
+            dma((PIECES * (size - 1),)),
             dma((size - 1,)),
             dma((size - 1,)),
         ],

time: 187 us -> 182 us (0.973)
  Pallas kernels: 182 us -> 177 us
    pallas_call x2, Pallas kernels: 101 us -> 96 us  [step(): pl.pallas_call(functools.partial(step_kernel, distance, times, size), out...]
where the time goes in v5:
time: 182 us
  Pallas kernels  177 us (97%)
  local copies, waits for them, and re-layouts  3.66 us (2%)
    pallas_call x2, Pallas kernels, step(): pl.pallas_call(functools.partial(step_kernel, distance, times, size), out...  96 us
    pallas_call x1, Pallas kernels, first(): pl.pallas_call(functools.partial(first_kernel, times, size), out_shape=(j...  50.3 us
    pallas_call x1, Pallas kernels, last(): pl.pallas_call(functools.partial(last_kernel, distance, times, size), out...  27.9 us

profile of v5, /device:TPU:0, one launch (start us, length us, event | category | flops | bytes accessed | tf_op | source)
XLA Modules:
  0.0 181.6 jit_solution(11672063300833524061)
XLA Ops:
  1.3 0.0 copy-start.1
  1.3 0.6 copy-done.1
  1.9 0.6 broadcast_in_dim.14.prior_ref
  2.5 2.3 %shard_map.68 = (bf16[384,512]{1,0:T(8,128)(2,1)}, bf16[384,512]{1,0:T(8,128)(2,1)}) custom-call(bf16[512,512]{1,0:T(8,128)(2,1)} %bitcast.5, bf16[128,512]{1,0:T(8,128)(2,1)} %bitcast.8, s32[1,4]{1,0:T(1,128)} %routes_ref.1, s32[1,1]{1,0:T(1,128)S(6)} %copy.9.counts_ref), custom_call_target="tpu_custom_call" | custom-call | tf_op jit(solution)/shard_map/pallas_call | solution.py:408
  4.9 50.3 %shard_map.69 = (f32[4,128,512]{2,1,0:T(8,128)}, f32[128,512]{1,0:T(8,128)}) custom-call(bf16[384,512]{1,0:T(8,128)(2,1)} %get-tuple-element.12.near_ref, bf16[384,512]{1,0:T(8,128)(2,1)} %get-tuple-element.13.sent_ref, f32[8,128]{1,0:T(8,128)} %broadcast_in_dim.14.prior_ref), custom_call_target="tpu_custom_call" | custom-call | tf_op jit(solution)/shard_map/pallas_call | solution.py:478
  55.2 45.8 %shard_map.70 = (f32[4,128,512]{2,1,0:T(8,128)}, f32[128,512]{1,0:T(8,128)}) custom-call(f32[4,128,512]{2,1,0:T(8,128)} %get-tuple-element.14.terms_ref, f32[128,512]{1,0:T(8,128)} %get-tuple-element.15.diag_ref), custom_call_target="tpu_custom_call" | custom-call | tf_op jit(solution)/shard_map/pallas_call | solution.py:313
  101.0 50.2 %shard_map.71 = (f32[4,128,512]{2,1,0:T(8,128)}, f32[128,512]{1,0:T(8,128)}) custom-call(f32[4,128,512]{2,1,0:T(8,128)} %get-tuple-element.16.terms_ref, f32[128,512]{1,0:T(8,128)} %get-tuple-element.17.diag_ref), custom_call_target="tpu_custom_call" | custom-call | tf_op jit(solution)/shard_map/pallas_call | solution.py:313
  151.2 27.9 %shard_map.72 = (f32[128,512]{1,0:T(8,128)}, f32[128,512]{1,0:T(8,128)}) custom-call(f32[4,128,512]{2,1,0:T(8,128)} %get-tuple-element.18.terms_ref, f32[128,512]{1,0:T(8,128)} %get-tuple-element.19.diag_ref), custom_call_target="tpu_custom_call" | custom-call | tf_op jit(solution)/shard_map/pallas_call | solution.py:362
  179.2 0.0 copy-start
  179.2 1.7 copy.10
  180.9 0.0 copy-done
  180.9 0.7 copy.11
Async XLA Ops:
  1.3 0.7 copy-start.1
  179.2 1.7 copy-start

commit v6 on v5

--- a/solution.py
+++ b/solution.py
@@ -8,7 +8,7 @@
 from jax.sharding import PartitionSpec as P
 
 LEVELS = 3
-PIECES = 2
+PIECES = 4
 
 
 def split(x):
@@ -419,9 +419,10 @@
     place, me, behind, ahead = greet(1, times, size, True)
     rows, order = diag_full.shape[1:]
     observed = near.shape[1] - rows
-    plan, start, receive, sent = handed(
-        me, 1, behind, ahead, [(sent_ref, far.at[place], True)], move_send, move_recv
-    )
+    piece = near.shape[1] // PIECES
+    cuts = [pl.ds(c * piece, piece) for c in range(PIECES)]
+    moves = [(sent_ref.at[cut], far.at[place, cut], True) for cut in cuts]
+    plan, start, receive, sent = handed(me, 1, behind, ahead, moves, move_send, move_recv)
     start(plan)
     near_spread = Spread(size, place, near, near_send, near_recv, near_ref)
     prior_spread = Spread(size, place, prior, prior_send, prior_recv, prior_ref)
@@ -429,14 +430,19 @@
     prior_spread.start_own()
     near[place] = near_ref[...]
     prior[place] = prior_ref[...]
-    receive(plan)
-    far_spread = Spread(size, place, far, far_send, far_recv)
-    far_spread.start_own()
+    far_spreads = []
+    for c, cut in enumerate(cuts):
+        receive(plan[c : c + 1])
+        far_spreads.append(
+            Spread(size, place, far, far_send, far_recv, None, cut, c * (size - 1))
+        )
+        far_spreads[c].start_own()
     near_spread.forward()
     prior_spread.forward()
     near_spread.finish()
     prior_spread.finish()
-    far_spread.forward()
+    for spread in far_spreads:
+        spread.forward()
     square = (rows, rows)
     unit = lax.broadcasted_iota(jnp.int32, square, 0) == lax.broadcasted_iota(jnp.int32, square, 1)
 
@@ -457,7 +463,8 @@
         diag_full[b] = total
         diag_full[b, :, cut] += jnp.where(unit, jnp.broadcast_to(prior[b][:1], square), 0.0)
         parts[b, 0] = near[b, observed:].astype(jnp.float32)
-    far_spread.finish()
+    for spread in far_spreads:
+        spread.finish()
     for b, cut, total in add_grams(far):
         diag_full[b] += total
         for q in range(size):
@@ -494,10 +501,11 @@
             pltpu.VMEM((size, rows, order), jnp.float32),
             pltpu.VMEM((order, 2 * order), jnp.bfloat16),
             pltpu.VMEM((order, 2 * order), jnp.bfloat16),
-            dma((1,)),
-            dma((1,)),
+            dma((PIECES,)),
+            dma((PIECES,)),
         ]
-        + [dma((size - 1,))] * 6,
+        + [dma((size - 1,))] * 4
+        + [dma((PIECES * (size - 1),))] * 2,
         compiler_params=pltpu.CompilerParams(collective_id=0, has_side_effects=True),
     )(near, sent, prior)
 

time: 182 us -> 178 us (0.978)
  Pallas kernels: 177 us -> 173 us
    pallas_call x2, Pallas kernels: 96 us -> 92.6 us  [step(): pl.pallas_call(functools.partial(step_kernel, distance, times, size), out...]
where the time goes in v6:
time: 178 us
  Pallas kernels  173 us (97%)
  local copies, waits for them, and re-layouts  3.66 us (2%)
    pallas_call x2, Pallas kernels, step(): pl.pallas_call(functools.partial(step_kernel, distance, times, size), out...  92.6 us
    pallas_call x1, Pallas kernels, first(): pl.pallas_call(functools.partial(first_kernel, times, size), out_shape=(j...  50.1 us
    pallas_call x1, Pallas kernels, last(): pl.pallas_call(functools.partial(last_kernel, distance, times, size), out...  27.9 us

profile of v6, /device:TPU:0, one launch (start us, length us, event | category | flops | bytes accessed | tf_op | source)
XLA Modules:
  0.0 178.0 jit_solution(9945644783844723789)
XLA Ops:
  1.3 0.0 copy-start.1
  1.3 0.6 copy-done.1
  1.9 0.6 broadcast_in_dim.14.prior_ref
  2.5 2.3 %shard_map.68 = (bf16[384,512]{1,0:T(8,128)(2,1)}, bf16[384,512]{1,0:T(8,128)(2,1)}) custom-call(bf16[512,512]{1,0:T(8,128)(2,1)} %bitcast.5, bf16[128,512]{1,0:T(8,128)(2,1)} %bitcast.8, s32[1,4]{1,0:T(1,128)} %routes_ref.1, s32[1,1]{1,0:T(1,128)S(6)} %copy.9.counts_ref), custom_call_target="tpu_custom_call" | custom-call | tf_op jit(solution)/shard_map/pallas_call | solution.py:408
  4.9 50.1 %shard_map.69 = (f32[4,128,512]{2,1,0:T(8,128)}, f32[128,512]{1,0:T(8,128)}) custom-call(bf16[384,512]{1,0:T(8,128)(2,1)} %get-tuple-element.12.near_ref, bf16[384,512]{1,0:T(8,128)(2,1)} %get-tuple-element.13.sent_ref, f32[8,128]{1,0:T(8,128)} %broadcast_in_dim.14.prior_ref), custom_call_target="tpu_custom_call" | custom-call | tf_op jit(solution)/shard_map/pallas_call | solution.py:485
  55.0 43.6 %shard_map.70 = (f32[4,128,512]{2,1,0:T(8,128)}, f32[128,512]{1,0:T(8,128)}) custom-call(f32[4,128,512]{2,1,0:T(8,128)} %get-tuple-element.14.terms_ref, f32[128,512]{1,0:T(8,128)} %get-tuple-element.15.diag_ref), custom_call_target="tpu_custom_call" | custom-call | tf_op jit(solution)/shard_map/pallas_call | solution.py:313
  98.7 49.0 %shard_map.71 = (f32[4,128,512]{2,1,0:T(8,128)}, f32[128,512]{1,0:T(8,128)}) custom-call(f32[4,128,512]{2,1,0:T(8,128)} %get-tuple-element.16.terms_ref, f32[128,512]{1,0:T(8,128)} %get-tuple-element.17.diag_ref), custom_call_target="tpu_custom_call" | custom-call | tf_op jit(solution)/shard_map/pallas_call | solution.py:313
  147.7 27.9 %shard_map.72 = (f32[128,512]{1,0:T(8,128)}, f32[128,512]{1,0:T(8,128)}) custom-call(f32[4,128,512]{2,1,0:T(8,128)} %get-tuple-element.18.terms_ref, f32[128,512]{1,0:T(8,128)} %get-tuple-element.19.diag_ref), custom_call_target="tpu_custom_call" | custom-call | tf_op jit(solution)/shard_map/pallas_call | solution.py:362
  175.6 0.0 copy-start
  175.6 1.7 copy.10
  177.3 0.0 copy-done
  177.3 0.7 copy.11
Async XLA Ops:
  1.3 0.7 copy-start.1
  175.6 1.7 copy-start
